TPU v7x, 32 devices: a whole 2x2x4 slice. The times are simulated.
32 devices in a mesh: dp: 2 (over y), expert: 16 (over z, x, core).
Axes of the slice: x: 2, y: 2, z: 4, core: 2. Of those that a mesh axis runs over, the one named last changes fastest.
Arguments:
- grad_out: bfloat16 [4096, 4096], P(('dp', 'expert')), may hold values from -6 to 6
- saved_pre: bfloat16 [4096, 2, 1536], P(('dp', 'expert')), may hold values from -6 to 6
- gate_weight: bfloat16 [4096, 2], P(('dp', 'expert')), may hold values from 0.049804688 to 0.59765625
- routes: int32 [4096, 2], P(('dp', 'expert')), may hold values from 0 to 15, all different within a row; in each aligned block of 128 rows (0 to 127, 128 to 255, ...) at most 20 rows name the same one
- w_down: bfloat16 [16, 768, 4096], P('expert', None, 'dp'), may hold values from -0.09375 to 0.09375
Outputs:
- grad_pre: bfloat16 [4096, 2, 1536], P(('dp', 'expert'))
- grad_gate: bfloat16 [4096, 2], P(('dp', 'expert'))
- grad_down: bfloat16 [16, 768, 4096], P('expert', None, 'dp')
Inputs may be any that keep to these rules, and one draw needn't show every extreme that they name: Among the routes of one device's 128 tokens no expert is named more than 20 times, a bound that some block reaches; a token names 2 different experts.
All inputs are finite; a program needn't handle non-finite values.
Results may differ from a plain program's by a relative error of at most 0.0085.
Values may be sent and summed in bfloat16 or wider, within the bound.
A program may use at most 128 MiB of HBM per device.

v0:
```python
import functools

import jax
import jax.numpy as jnp
from jax import lax
from jax.experimental import pallas as pl
from jax.experimental.pallas import tpu as pltpu
from jax.sharding import PartitionSpec as P

BF16 = jnp.bfloat16
F32 = jnp.float32


def slot_positions(routes_flat, experts, capacity):
    expert_ids = jnp.arange(experts, dtype=jnp.int32)
    onehot = (routes_flat[:, None] == expert_ids[None, :]).astype(jnp.int32)
    rank = jnp.sum((jnp.cumsum(onehot, axis=0) - 1) * onehot, axis=1)
    return routes_flat * capacity + rank


def swiglu_parts(saved, hidden):
    gate_pre = saved[..., :hidden].astype(F32)
    up_pre = saved[..., hidden:].astype(F32)
    return (gate_pre, up_pre, jax.nn.silu(gate_pre))


def swiglu_grads(saved, weights, contraction, hidden):
    gate_pre, up_pre, active = swiglu_parts(saved, hidden)
    plain = (active * up_pre).astype(BF16)
    gate_grad = jnp.sum(plain.astype(F32) * contraction.astype(F32), axis=-1).astype(BF16)
    back = weights.astype(F32)[..., None] * contraction.astype(F32)
    sigma = jax.nn.sigmoid(gate_pre)
    grad_gate_pre = back * up_pre * sigma * (1.0 + gate_pre * (1.0 - sigma))
    grad_up_pre = back * active
    return (jnp.concatenate([grad_gate_pre, grad_up_pre], axis=-1).astype(BF16), gate_grad)


def scaled_hidden(saved, weights, hidden):
    gate_pre, up_pre, active = swiglu_parts(saved, hidden)
    return (weights.astype(F32)[..., None] * active * up_pre).astype(BF16)


def dot(a, b, dims):
    return lax.dot_general(a, b, (dims, ((), ())), preferred_element_type=F32)


def on_device_general(grad_out, saved_pre, gate_weight, routes, w_down):
    tokens_dev, top_count = routes.shape
    hidden = w_down.shape[1]
    half = w_down.shape[2]
    experts = lax.axis_size("expert")
    replicas = lax.axis_size("dp")
    capacity = 5 * tokens_dev * top_count // (4 * experts)
    slots = experts * capacity
    positions = slot_positions(routes.reshape(-1), experts, capacity).reshape(tokens_dev, top_count)
    slot_ids = jnp.arange(slots, dtype=jnp.int32)
    picks = [
        (positions[:, k][None, :] == slot_ids[:, None]).astype(BF16) for k in range(top_count)
    ]
    pick = sum(picks[1:], picks[0])
    devices = replicas * experts
    send_rows = jnp.stack(
        [
            dot(pick, grad_out[:, d * half : (d + 1) * half], ((1,), (0,))).astype(BF16)
            for d in range(replicas)
        ]
    ).reshape(devices, capacity, half)
    scaled = scaled_hidden(saved_pre, gate_weight, hidden)
    send_scaled = sum(dot(picks[k], scaled[:, k], ((1,), (0,))) for k in range(top_count))
    send_scaled = send_scaled.astype(BF16).reshape(experts, capacity, hidden)
    rows = lax.all_to_all(send_rows, ("dp", "expert"), split_axis=0, concat_axis=0, tiled=True)
    scaled_in = lax.all_to_all(send_scaled, "expert", split_axis=0, concat_axis=0, tiled=True)
    scaled_in = lax.all_gather(scaled_in.reshape(slots, hidden), "dp", axis=0, tiled=True)
    rows = rows.reshape(devices * capacity, half)
    partial = dot(rows, w_down[0], ((1,), (1,))).astype(BF16).reshape(devices, capacity, hidden)
    parts = lax.all_to_all(partial, ("dp", "expert"), split_axis=0, concat_axis=0, tiled=True)
    parts = parts.reshape(replicas, slots, hidden)
    contraction = jnp.stack(
        [
            sum(dot(picks[k], parts[d], ((0,), (0,))) for d in range(replicas))
            for k in range(top_count)
        ],
        axis=1,
    ).astype(BF16)
    grads, gate_grad = swiglu_grads(saved_pre, gate_weight, contraction, hidden)
    grad_down = dot(scaled_in, rows, ((0,), (0,))).astype(BF16)
    return grads, gate_grad, grad_down[None]


BASE = 16
MESH = pl.DeviceIdType.MESH


def iota(shape, axis):
    return lax.broadcasted_iota(jnp.int32, shape, axis)


def unfold_pick(groups, rest, fold, q):
    shape = (groups * rest, groups * BASE)
    row, col = iota(shape, 0), iota(shape, 1)
    return (col == (row // rest) * BASE + q * rest + row % rest).astype(BF16)


def fold_pick(groups, rest, fold, q):
    shape = (groups * BASE, groups * rest)
    row, col = iota(shape, 0), iota(shape, 1)
    mine = (row // rest) % fold == q
    return (mine & (col == (row // BASE) * rest + row % rest)).astype(BF16)


def pack(
    experts, rest, fold, replicas, s_fold,
    routes, rows, scaled0, scaled1,
    main, left, smain, sleft, pos,
):
    tokens, width = rows.shape
    half = width // replicas
    part = half // fold
    count = experts * BASE
    names = iota((experts, tokens), 0)
    named = [(routes[k : k + 1, :] == names).astype(F32) for k in range(2)]
    before = (iota((tokens, tokens), 0) < iota((tokens, tokens), 1)).astype(BF16)
    counts = dot((named[0] + named[1]).astype(BF16), before, ((1,), (0,)))
    for k in range(2):
        rank = jnp.sum(counts * named[k], axis=0, keepdims=True).astype(jnp.int32)
        expert = routes[k : k + 1, :]
        pos[k : k + 1, :] = jnp.where(
            rank < BASE, expert * BASE + rank, count + expert * rest + rank - BASE
        )
    pos0, pos1 = pos[0:1, :], pos[1:2, :]
    row = iota((count, tokens), 0)
    pick0, pick1 = (pos0 == row).astype(BF16), (pos1 == row).astype(BF16)
    both = pick0 + pick1
    step = 1024
    for c in range(0, width, step):
        main[:, c : c + step] = dot(both, rows[:, c : c + step], ((1,), (0,))).astype(BF16)
    smain[...] = (
        dot(pick0, scaled0[...], ((1,), (0,))) + dot(pick1, scaled1[...], ((1,), (0,)))
    ).astype(BF16)
    slot = count + (row // BASE) * rest + row % rest
    total = [jnp.zeros((count, part), F32) for _ in range(replicas)]
    part_s = sleft.shape[1]
    total_s = jnp.zeros((count, part_s), F32)
    for q in range(fold):
        mine = (row // rest) % fold == q
        q0, q1 = ((pos0 == slot) & mine).astype(BF16), ((pos1 == slot) & mine).astype(BF16)
        for d in range(replicas):
            at = d * half + q * part
            total[d] = total[d] + dot(q0 + q1, rows[:, at : at + part], ((1,), (0,)))
        if q < s_fold:
            at = q * part_s
            total_s = total_s + dot(q0, scaled0[:, at : at + part_s], ((1,), (0,)))
            total_s = total_s + dot(q1, scaled1[:, at : at + part_s], ((1,), (0,)))
    for d in range(replicas):
        left[:, d * part : (d + 1) * part] = total[d].astype(BF16)
    sleft[...] = total_s.astype(BF16)


def exchange_kernel(
    experts, rest, fold, s_fold,
    routes, rows_in, scaled0, scaled1, w_hbm,
    ret_out, grad_out, pos,
    main, left, smain, sleft, w, x_main, x_left, z, s_main, s_left, s_rest, s_turn, s_turn_rest,
    mine_f32, out_px, in_px, out_pl, in_pl, c_main, c_left, r_main, r_left,
    w_sem, tx, rx, txl, rxl, ts, rs, tsl, rsl, tp, rp, tc, rc, tcl, rcl,
):
    d = lax.axis_index("dp")
    e = lax.axis_index("expert")
    other = 1 - d
    devices = 2 * experts
    me = d * experts + e
    half = w.shape[1]
    part = half // fold
    hidden = w.shape[0]
    part_s = sleft.shape[1]
    own, rest_own = experts * BASE, experts * rest

    def block(i):
        return pl.ds(pl.multiple_of(i * BASE, BASE), BASE)

    def remote(src, dst, send, recv, to):
        return pltpu.make_async_remote_copy(
            src_ref=src, dst_ref=dst, send_sem=send, recv_sem=recv, device_id=to, device_id_type=MESH
        )

    def row_copies(p, s):
        pd, pe = p // experts, p % experts
        wide = pl.ds(pl.multiple_of(pd * half, 128), half)
        narrow = pl.ds(pl.multiple_of(pd * part, 128), part)
        return (
            remote(main.at[block(pe), wide], x_main.at[block(s)], tx.at[p], rx.at[s], (pd, pe)),
            remote(left.at[block(pe), narrow], x_left.at[block(s)], txl.at[p], rxl.at[s], (pd, pe)),
        )

    def scaled_copies(pe, se):
        s = d * experts + se
        return (
            remote(smain.at[block(pe)], s_main.at[block(s)], ts.at[pe], rs.at[se], (d, pe)),
            remote(sleft.at[block(pe)], s_left.at[block(s)], tsl.at[pe], rsl.at[se], (d, pe)),
        )

    def back_copies(pe, se):
        return (
            remote(c_main.at[block(pe)], r_main.at[block(se)], tc.at[pe], rc.at[se], (d, pe)),
            remote(c_left.at[block(pe)], r_left.at[block(se)], tcl.at[pe], rcl.at[se], (d, pe)),
        )

    def each(count, position, body):
        def step(k, carry):
            body((position + 1 + (k + count // 2 - 1) % (count - 1)) % count)
            return carry

        lax.fori_loop(1, count, step, 0)

    fetch_w = pltpu.make_async_copy(w_hbm, w, w_sem)
    fetch_w.start()
    barrier = pltpu.get_barrier_semaphore()

    def greet(p):
        pl.semaphore_signal(
            barrier, inc=1, device_id=(p // experts, p % experts), device_id_type=MESH
        )

    each(devices, me, greet)
    pack(
        experts, rest, fold, 2, s_fold,
        routes, rows_in, scaled0, scaled1,
        main, left, smain, sleft, pos,
    )
    pl.semaphore_wait(barrier, devices - 1)

    def start_across(k, carry):
        for copy in row_copies(other * experts + (e + experts // 2 + k) % experts, me):
            copy.start()
        return carry

    lax.fori_loop(0, experts, start_across, 0)

    def start_scaled(p):
        for copy in scaled_copies(p, e):
            copy.start()

    each(experts, e, start_scaled)

    def start_rows(p):
        for copy in row_copies(d * experts + p, me):
            copy.start()

    each(experts, e, start_rows)
    kept = [
        pltpu.make_async_copy(
            main.at[block(e), pl.ds(pl.multiple_of(d * half, 128), half)], x_main.at[block(me)], rx.at[me]
        ),
        pltpu.make_async_copy(
            left.at[block(e), pl.ds(pl.multiple_of(d * part, 128), part)], x_left.at[block(me)], rxl.at[me]
        ),
        pltpu.make_async_copy(smain.at[block(e)], s_main.at[block(me)], rs.at[e]),
        pltpu.make_async_copy(sleft.at[block(e)], s_left.at[block(me)], rsl.at[e]),
    ]
    for copy in kept:
        copy.start()
    for copy in kept:
        copy.wait()
    fetch_w.wait()

    other_at, own_at = pl.multiple_of(other * own, own), pl.multiple_of(d * own, own)
    other_rest, own_rest = pl.multiple_of(other * rest_own, rest_own), pl.multiple_of(d * rest_own, rest_own)

    def unfold_rows(at, rest_at):
        for q in range(fold):
            z[pl.ds(rest_at, rest_own), q * part : (q + 1) * part] = dot(
                unfold_pick(experts, rest, fold, q), x_left[pl.ds(at, own), :], ((1,), (0,))
            ).astype(BF16)

    def contract(lo, ref, rows, start):
        return dot(ref[pl.ds(start, rows), :], w[lo : lo + 256, :], ((1,), (1,)))

    def wait_across(k, carry):
        s = other * experts + k
        for copy in row_copies(s, s):
            copy.wait_recv()
        return carry

    lax.fori_loop(0, experts, wait_across, 0)
    unfold_rows(other_at, other_rest)
    for lo in range(0, hidden, 256):
        out_px[:, lo : lo + 256] = contract(lo, x_main, own, other_at).astype(BF16)
        out_pl[:, lo : lo + 256] = contract(lo, z, rest_own, other_rest).astype(BF16)
    across = (other, e)
    px = remote(out_px, in_px, tp.at[0], rp.at[0], across)
    plx = remote(out_pl, in_pl, tp.at[1], rp.at[1], across)
    px.start()
    plx.start()

    def wait_scaled(s):
        for copy in scaled_copies(s, s):
            copy.wait_recv()

    each(experts, e, wait_scaled)
    region = pl.ds(own_at, own)
    forward = [
        remote(s_main.at[region], s_main.at[region], tp.at[2], rp.at[2], across),
        remote(s_left.at[region], s_left.at[region], tp.at[3], rp.at[3], across),
    ]
    for copy in forward:
        copy.start()
    px.wait()
    plx.wait()
    for copy in forward:
        copy.wait()
    for q in range(s_fold):
        s_rest[:, q * part_s : (q + 1) * part_s] = dot(
            unfold_pick(devices, rest, fold, q), s_left[...], ((1,), (0,))
        ).astype(BF16)
    s_turn[...] = s_main[...].T
    s_turn_rest[...] = s_rest[...].T

    def wait_rows(p):
        s = d * experts + p
        for copy in row_copies(s, s):
            copy.wait_recv()

    each(experts, e, wait_rows)
    unfold_rows(own_at, own_rest)
    for lo in range(0, hidden, 256):
        cut = slice(lo, lo + 256)
        c_main[:, cut] = (contract(lo, x_main, own, own_at) + in_px[:, cut].astype(F32)).astype(BF16)
        mine_f32[:, cut] = contract(lo, z, rest_own, own_rest)
    c_rest = (mine_f32[...] + in_pl[...].astype(F32)).astype(BF16)
    folded = jnp.zeros((own, part_s), F32)
    for q in range(s_fold):
        folded = folded + dot(
            fold_pick(experts, rest, fold, q), c_rest[:, q * part_s : (q + 1) * part_s], ((1,), (0,))
        )
    c_left[...] = folded.astype(BF16)

    def start_back(p):
        for copy in back_copies(p, e):
            copy.start()

    each(experts, e, start_back)
    kept_back = [
        pltpu.make_async_copy(c_main.at[block(e)], r_main.at[block(e)], rc.at[e]),
        pltpu.make_async_copy(c_left.at[block(e)], r_left.at[block(e)], rcl.at[e]),
    ]
    for copy in kept_back:
        copy.start()

    @pl.loop(0, half // 512)
    def _(j):
        columns = pl.ds(pl.multiple_of(j * 512, 512), 512)
        grad_out[:, columns] = (
            dot(s_turn[...], x_main[:, columns], ((1,), (0,)))
            + dot(s_turn_rest[...], z[:, columns], ((1,), (0,)))
        ).astype(BF16)

    for copy in kept_back:
        copy.wait()

    def wait_back(s):
        for copy in back_copies(s, s):
            copy.wait_recv()

    each(experts, e, wait_back)
    ret_out[0:own, :] = r_main[...]
    for q in range(s_fold):
        ret_out[own : own + rest_own, q * part_s : (q + 1) * part_s] = dot(
            unfold_pick(experts, rest, fold, q), r_left[...], ((1,), (0,))
        ).astype(BF16)

    def drain_rows(p):
        for copy in row_copies(p, me):
            copy.wait_send()

    each(devices, me, drain_rows)

    def drain(p):
        for copy in scaled_copies(p, e) + back_copies(p, e):
            copy.wait_send()

    each(experts, e, drain)


def on_device(grad_out, saved_pre, gate_weight, routes, w_down):
    tokens, top_count = routes.shape
    hidden, half = w_down.shape[1:]
    width = grad_out.shape[1]
    experts = lax.axis_size("expert")
    replicas = lax.axis_size("dp")
    capacity = 5 * tokens * top_count // (4 * experts)
    if (replicas, top_count, capacity, hidden % 256, half % 512) != (2, 2, 20, 0, 0):
        return on_device_general(grad_out, saved_pre, gate_weight, routes, w_down)
    rest = capacity - BASE
    fold = BASE // rest
    s_fold = hidden // 256
    own, rest_own = experts * BASE, experts * rest
    devices = replicas * experts
    scaled = [
        scaled_hidden(saved_pre[:, k], gate_weight[:, k], hidden) for k in range(2)
    ]
    vmem = pl.BlockSpec(memory_space=pltpu.VMEM)
    dma = pltpu.SemaphoreType.DMA
    total = devices * BASE
    back, grad_down, positions = pl.pallas_call(
        functools.partial(exchange_kernel, experts, rest, fold, s_fold),
        out_shape=(
            jax.ShapeDtypeStruct((own + rest_own, hidden), BF16),
            jax.ShapeDtypeStruct((hidden, half), BF16),
            jax.ShapeDtypeStruct((2, tokens), jnp.int32),
        ),
        in_specs=[vmem] * 4 + [pl.BlockSpec(memory_space=pl.ANY)],
        out_specs=[vmem] * 3,
        scratch_shapes=[
            pltpu.VMEM((own, width), BF16),
            pltpu.VMEM((own, width // fold), BF16),
            pltpu.VMEM((own, hidden), BF16),
            pltpu.VMEM((own, 256), BF16),
            pltpu.VMEM((hidden, half), BF16),
            pltpu.VMEM((total, half), BF16),
            pltpu.VMEM((total, half // fold), BF16),
            pltpu.VMEM((devices * rest, half), BF16),
            pltpu.VMEM((total, hidden), BF16),
            pltpu.VMEM((total, 256), BF16),
            pltpu.VMEM((devices * rest, hidden), BF16),
            pltpu.VMEM((hidden, total), BF16),
            pltpu.VMEM((hidden, devices * rest), BF16),
            pltpu.VMEM((rest_own, hidden), F32),
            pltpu.VMEM((own, hidden), BF16),
            pltpu.VMEM((own, hidden), BF16),
            pltpu.VMEM((rest_own, hidden), BF16),
            pltpu.VMEM((rest_own, hidden), BF16),
            pltpu.VMEM((own, hidden), BF16),
            pltpu.VMEM((own, 256), BF16),
            pltpu.VMEM((own, hidden), BF16),
            pltpu.VMEM((own, 256), BF16),
            dma,
            dma((devices,)), dma((devices,)), dma((devices,)), dma((devices,)),
            dma((experts,)), dma((experts,)), dma((experts,)), dma((experts,)),
            dma((4,)), dma((4,)),
            dma((experts,)), dma((experts,)), dma((experts,)), dma((experts,)),
        ],
        compiler_params=pltpu.CompilerParams(collective_id=0, has_side_effects=True),
    )(routes.T, grad_out, scaled[0], scaled[1], w_down[0])
    slot_ids = jnp.arange(own + rest_own, dtype=jnp.int32)
    pick = (positions[:, :, None] == slot_ids).astype(BF16).reshape(2 * tokens, -1)
    contraction = dot(pick, back, ((1,), (0,))).astype(BF16).reshape(2, tokens, hidden)
    contraction = jnp.stack([contraction[0], contraction[1]], axis=1)
    grads, gate_grad = swiglu_grads(saved_pre, gate_weight, contraction, hidden)
    return grads, gate_grad, grad_down[None]


def solution(mesh):
    return jax.shard_map(
        on_device,
        mesh=mesh,
        in_specs=(
            P(("dp", "expert"), None),
            P(("dp", "expert"), None, None),
            P(("dp", "expert"), None),
            P(("dp", "expert"), None),
            P("expert", None, "dp"),
        ),
        out_specs=(
            P(("dp", "expert"), None, None),
            P(("dp", "expert"), None),
            P("expert", None, "dp"),
        ),
        check_vma=False,
    )
```

profile of v0, /device:TPU:0, one launch (start us, length us, event | category | flops | bytes accessed | tf_op | source)
XLA Modules:
  0.0 115.8 jit_solution(4287582204536751156)
XLA Ops:
  0.6 0.7 convert_element_type.49
  1.3 0.7 bitcast_convert_fusion
  2.0 1.7 %fusion.24 = (bf16[128,2,768]{2,1,0:T(2,128)(2,1)S(1)}, bf16[128,2,768]{2,1,0:T(2,128)(2,1)S(1)}) fusion(bf16[128,2,1536]{2,1,0:T(2,128)(2,1)} %param.6), kind=kLoop, calls=%fused_computation.45 | loop fusion | bytes 1572864 | tf_op jit(solution)/shard_map/slice | solution.py:23
  3.7 2.7 %fusion.25 = (bf16[128,1,1536]{2,1,0:T(2,128)(2,1)S(1)}, bf16[128,1,1536]{2,1,0:T(2,128)(2,1)S(1)}) fusion(bf16[128,2,1536]{2,1,0:T(2,128)(2,1)} %param.6), kind=kLoop, calls=%fused_computation.46 | loop fusion | bytes 1572864 | tf_op jit(solution)/shard_map/slice | solution.py:399
  6.4 0.1 copy_bitcast_fusion
  6.5 0.8 fusion.21.scaled1
  7.4 0.8 fusion.22.scaled0
  8.2 101.5 %shard_map.76 = (bf16[320,768]{1,0:T(8,128)(2,1)}, bf16[768,2048]{1,0:T(8,128)(2,1)}, s32[2,128]{1,0:T(2,128)}) custom-call(s32[2,128]{1,0:T(2,128)} %bitcast.21, bf16[128,4096]{1,0:T(8,128)(2,1)} %rows_in.1, bf16[128,768]{1,0:T(8,128)(2,1)} %fusion.22.scaled0, bf16[128,768]{1,0:T(8,128)(2,1)} %fusion.21.scaled1, bf16[768,2048]{1,0:T(8,128)(2,1)} %bitcast.19), custom_call_target="tpu_custom_call" | custom-call | tf_op jit(solution)/shard_map/pallas_call | solution.py:404
  109.7 1.4 %convolution_convert_fusion = bf16[256,768]{1,0:T(8,128)(2,1)S(1)} fusion(bf16[320,768]{1,0:T(8,128)(2,1)} %get-tuple-element.7, s32[256]{0:T(256)} %bitcast.22), kind=kOutput, calls=%fused_computation | convolution fusion | flops 126107648 | bytes 885760 | tf_op jit(solution)/shard_map/dot_general | solution.py:44
  111.1 0.0 copy-start
  111.2 1.2 %fusion.2 = (bf16[128,2]{0,1:T(2,128)(2,1)}, bf16[128,2,768]{2,0,1:T(8,128)(2,1)S(1)}, bf16[128,2,768]{2,0,1:T(8,128)(2,1)S(1)}) fusion(bf16[128,2,768]{2,1,0:T(2,128)(2,1)S(1)} %get-tuple-element.15, bf16[128,2,768]{2,1,0:T(2,128)(2,1)S(1)} %get-tuple-element.16, bf16[128,1,768]{2,0,1:T(8,128)(2,1)S(1)} %get-tuple-element.20, ...), kind=kLoop, calls=%fused_computation.10 | loop fusion | flops 4914944 | bytes 1967616 | tf_op jit(solution)/shard_map/reduce_sum | solution.py:30
  112.4 0.1 pad_maximum_fusion
  112.4 1.7 %copy.12 = bf16[128,2,1536]{2,1,0:T(2,128)(2,1)} copy(bf16[128,2,1536]{2,0,1:T(8,128)(2,1)S(1)} %pad_maximum_fusion) | data formatting | bytes 1572864
  114.1 0.0 copy-done
  114.1 1.7 %copy.28 = bf16[1,768,2048]{2,1,0:T(8,128)(2,1)} copy(bf16[1,768,2048]{2,1,0:T(8,128)(2,1)S(1)} %bitcast.20) | data formatting | bytes 6291456
  (1 shorter events, 0.0 us)
Async XLA Ops:
  111.1 3.0 %copy-start = (bf16[768,2048]{1,0:T(8,128)(2,1)S(1)}, bf16[768,2048]{1,0:T(8,128)(2,1)}, u32[]{:S(2)}) copy-start(bf16[768,2048]{1,0:T(8,128)(2,1)} %get-tuple-element.8) | copy-start | bytes 9437188
where the time goes:
time: 116 us
  Pallas kernels  101 us (87%)
  local copies, waits for them, and re-layouts  7.87 us (7%)
  other arithmetic  4.33 us (4%)
  matrix products  1.44 us (1%)
    pallas_call x1, Pallas kernels, on_device(): pl.pallas_call(functools.partial(exchange_kernel, experts, rest, fold, s_...  101 us
    unnamed x4, local copies, waits for them, and re-layouts  3.36 us
    slice x1, local copies, waits for them, and re-layouts, on_device(): saved_pre[:, k]  2.72 us

commit v1 on v0

v1 whole, which is shorter than its diff:
```python
import functools

import jax
import jax.numpy as jnp
from jax import lax
from jax.experimental import pallas as pl
from jax.experimental.pallas import tpu as pltpu
from jax.sharding import PartitionSpec as P

BF16 = jnp.bfloat16
F32 = jnp.float32


def slot_positions(routes_flat, experts, capacity):
    expert_ids = jnp.arange(experts, dtype=jnp.int32)
    onehot = (routes_flat[:, None] == expert_ids[None, :]).astype(BF16)
    ids = jnp.arange(routes_flat.shape[0], dtype=jnp.int32)
    before = (ids[None, :] < ids[:, None]).astype(BF16)
    counts = dot(before, onehot, ((1,), (0,)))
    rank = jnp.sum(counts * onehot.astype(F32), axis=1).astype(jnp.int32)
    return routes_flat * capacity + rank


def swiglu_parts(saved, hidden):
    gate_pre = saved[..., :hidden].astype(F32)
    up_pre = saved[..., hidden:].astype(F32)
    return (gate_pre, up_pre, jax.nn.silu(gate_pre))


def swiglu_grads(saved, weights, contraction, hidden):
    gate_pre, up_pre, active = swiglu_parts(saved, hidden)
    plain = (active * up_pre).astype(BF16)
    gate_grad = jnp.sum(plain.astype(F32) * contraction.astype(F32), axis=-1).astype(BF16)
    back = weights.astype(F32)[..., None] * contraction.astype(F32)
    sigma = jax.nn.sigmoid(gate_pre)
    grad_gate_pre = back * up_pre * sigma * (1.0 + gate_pre * (1.0 - sigma))
    grad_up_pre = back * active
    return (jnp.concatenate([grad_gate_pre, grad_up_pre], axis=-1).astype(BF16), gate_grad)


def scaled_hidden(saved, weights, hidden):
    gate_pre, up_pre, active = swiglu_parts(saved, hidden)
    return (weights.astype(F32)[..., None] * active * up_pre).astype(BF16)


def dot(a, b, dims):
    return lax.dot_general(a, b, (dims, ((), ())), preferred_element_type=F32)


def on_device_general(grad_out, saved_pre, gate_weight, routes, w_down):
    tokens_dev, top_count = routes.shape
    hidden = w_down.shape[1]
    half = w_down.shape[2]
    experts = lax.axis_size("expert")
    replicas = lax.axis_size("dp")
    capacity = 5 * tokens_dev * top_count // (4 * experts)
    slots = experts * capacity
    positions = slot_positions(routes.reshape(-1), experts, capacity).reshape(tokens_dev, top_count)
    slot_ids = jnp.arange(slots, dtype=jnp.int32)
    picks = [
        (positions[:, k][None, :] == slot_ids[:, None]).astype(BF16) for k in range(top_count)
    ]
    pick = sum(picks[1:], picks[0])
    devices = replicas * experts
    send_rows = jnp.stack(
        [
            dot(pick, grad_out[:, d * half : (d + 1) * half], ((1,), (0,))).astype(BF16)
            for d in range(replicas)
        ]
    ).reshape(devices, capacity, half)
    scaled = scaled_hidden(saved_pre, gate_weight, hidden)
    send_scaled = sum(dot(picks[k], scaled[:, k], ((1,), (0,))) for k in range(top_count))
    send_scaled = send_scaled.astype(BF16).reshape(experts, capacity, hidden)
    rows = lax.all_to_all(send_rows, ("dp", "expert"), split_axis=0, concat_axis=0, tiled=True)
    scaled_in = lax.all_to_all(send_scaled, "expert", split_axis=0, concat_axis=0, tiled=True)
    scaled_in = lax.all_gather(scaled_in.reshape(slots, hidden), "dp", axis=0, tiled=True)
    rows = rows.reshape(devices * capacity, half)
    partial = dot(rows, w_down[0], ((1,), (1,))).astype(BF16).reshape(devices, capacity, hidden)
    parts = lax.all_to_all(partial, ("dp", "expert"), split_axis=0, concat_axis=0, tiled=True)
    parts = parts.reshape(replicas, slots, hidden)
    contraction = jnp.stack(
        [
            sum(dot(picks[k], parts[d], ((0,), (0,))) for d in range(replicas))
            for k in range(top_count)
        ],
        axis=1,
    ).astype(BF16)
    grads, gate_grad = swiglu_grads(saved_pre, gate_weight, contraction, hidden)
    grad_down = dot(scaled_in, rows, ((0,), (0,))).astype(BF16)
    return grads, gate_grad, grad_down[None]


BASE = 16
MESH = pl.DeviceIdType.MESH


def iota(shape, axis):
    return lax.broadcasted_iota(jnp.int32, shape, axis)


def unfold_pick(groups, rest, q):
    shape = (groups * rest, groups * BASE)
    row, col = iota(shape, 0), iota(shape, 1)
    return (col == (row // rest) * BASE + q * rest + row % rest).astype(BF16)


def fold_pick(groups, rest, fold, q):
    shape = (groups * BASE, groups * rest)
    row, col = iota(shape, 0), iota(shape, 1)
    mine = (row // rest) % fold == q
    return (mine & (col == (row // BASE) * rest + row % rest)).astype(BF16)


def slot_keys(experts, rest, far, routes):
    tokens = routes.shape[1]
    names = iota((experts, tokens), 0)
    relative = [(routes[k : k + 1, :] + experts - far) % experts for k in range(2)]
    named = [(relative[k] == names).astype(F32) for k in range(2)]
    before = (iota((tokens, tokens), 0) < iota((tokens, tokens), 1)).astype(BF16)
    counts = dot((named[0] + named[1]).astype(BF16), before, ((1,), (0,)))
    keys = []
    for k in range(2):
        rank = jnp.sum(counts * named[k], axis=0, keepdims=True).astype(jnp.int32)
        keys.append(
            (
                jnp.where(rank < BASE, relative[k] * BASE + rank, -1),
                jnp.where(rank < BASE, -1, relative[k] * rest + rank - BASE),
            )
        )
    return keys


def exchange_kernel(
    experts, rest, fold, s_fold,
    routes, weights, rows_hbm, saved_hbm, w_hbm,
    pre_out, gate_out, down_hbm,
    rows, saved, w, pack, x, z, scaled, s_pack, s, s_rest, s_turn, px_out, px_in, c, r, c_routes,
    grad_gate_factor, grad_up_factor, plain, key_col, left_col, weight_col, gate_col, total, down,
    load_sem, down_sem, ts, rs, tss, rss, tf, rf, tp, rp, tb, rb,
):
    d = lax.axis_index("dp")
    e = lax.axis_index("expert")
    other = 1 - d
    me = d * experts + e
    half_experts = experts // 2
    at = e % half_experts
    near = (e // half_experts) * half_experts
    far = half_experts - near
    tokens, width = rows.shape
    half = width // 2
    part = half // fold
    hidden = w.shape[0]
    part_s = hidden // s_fold
    group = half_experts * BASE
    rest_group = half_experts * rest
    count = experts * BASE

    def block(i):
        return pl.ds(pl.multiple_of(i * BASE, BASE), BASE)

    def remote(src, dst, send, recv, to):
        return pltpu.make_async_remote_copy(
            src_ref=src, dst_ref=dst, send_sem=send, recv_sem=recv, device_id=to, device_id_type=MESH
        )

    def wait_bytes(ref, sem):
        pltpu.make_async_copy(ref, ref, sem).wait()

    def loop(first, last, body):
        def step(k, carry):
            body(k)
            return carry

        lax.fori_loop(first, last, step, 0)

    loads = [
        pltpu.make_async_copy(rows_hbm, rows, load_sem.at[0]),
        pltpu.make_async_copy(saved_hbm, saved, load_sem.at[1]),
        pltpu.make_async_copy(w_hbm, w, load_sem.at[2]),
    ]
    for load in loads:
        load.start()
    barrier = pltpu.get_barrier_semaphore()

    def greet(k):
        p = (me + k) % (2 * experts)
        pl.semaphore_signal(
            barrier, inc=1, device_id=(p // experts, p % experts), device_id_type=MESH
        )

    loop(1, 2 * experts, greet)

    (key0, left0), (key1, left1) = slot_keys(experts, rest, far, routes[...])
    row = iota((count, tokens), 0)
    main_pick = ((key0 == row) | (key1 == row)).astype(BF16)
    slot = (row // BASE) * rest + row % rest
    hit = (left0 == slot) | (left1 == slot)
    left_pick = jnp.concatenate(
        [(hit & ((row // rest) % fold == q)).astype(BF16) for q in range(fold)], axis=1
    )

    def pack_half(side, h):
        def columns(lo, size):
            return pl.ds(pl.multiple_of(h * half + lo, part), size)

        for lo in range(0, half, 512):
            pack[side, :, lo : lo + 512] = dot(
                main_pick, rows[:, columns(lo, 512)], ((1,), (0,))
            ).astype(BF16)
        folded = jnp.concatenate([rows[:, columns(q * part, part)] for q in range(fold)], axis=0)
        pack[side, :, half : half + part] = dot(left_pick, folded, ((1,), (0,))).astype(BF16)

    def row_copy(side, is_far, j):
        g = (0 if is_far else 2) + side
        source = pack.at[side, block(j if is_far else half_experts + j)]
        to = (other if side == 0 else d, (far if is_far else near) + j)
        return remote(source, x.at[block(g * half_experts + at)], ts.at[g], rs.at[g], to)

    loads[0].wait()
    pack_half(0, other)
    pl.semaphore_wait(barrier, 2 * experts - 1)

    def start_across(k):
        j = (at + k) % half_experts
        row_copy(0, True, j).start()
        row_copy(0, False, j).start()

    loop(0, half_experts, start_across)
    pack_half(1, d)

    def start_own(k):
        j = (at + k) % half_experts
        row_copy(1, True, j).start()
        row_copy(1, False, j).start()

    row_copy(1, True, at).start()
    loop(1, half_experts, start_own)
    pltpu.make_async_copy(
        pack.at[1, block(half_experts + at)], x.at[block(3 * half_experts + at)], rs.at[3]
    ).start()

    token_of = iota((2 * tokens, tokens), 0) // 2 == iota((2 * tokens, tokens), 1)
    first = iota((2 * tokens, tokens), 0) % 2 == 0

    def column(v0, v1):
        value = jnp.where(first, v0.astype(F32), v1.astype(F32))
        return jnp.sum(jnp.where(token_of, value, 0.0), axis=1, keepdims=True)

    key_col[...] = column(key0, key1).astype(jnp.int32)
    left_col[...] = column(left0, left1).astype(jnp.int32)
    weight_col[...] = column(weights[0:1, :], weights[1:2, :])
    loads[1].wait()
    step = 16

    @pl.loop(0, tokens // step)
    def _(i):
        mine = pl.ds(pl.multiple_of(i * 2 * step, 2 * step), 2 * step)
        both = saved[pl.ds(pl.multiple_of(i * step, step), step)].reshape(2 * step, 2 * hidden)
        gate_pre = both[:, :hidden].astype(F32)
        up_pre = both[:, hidden:].astype(F32)
        sigma = jax.nn.sigmoid(gate_pre)
        active = gate_pre * sigma
        weight = weight_col[mine, :]
        plain[mine, :] = (active * up_pre).astype(BF16)
        scaled[mine, :] = (weight * active * up_pre).astype(BF16)
        grad_up_factor[mine, :] = weight * active
        grad_gate_factor[mine, :] = weight * up_pre * sigma * (1.0 + gate_pre * (1.0 - sigma))

    slots = iota((2 * tokens, count), 1)

    def route_pick():
        return (key_col[...] == slots).astype(BF16)

    def route_left(q):
        wanted = (slots // BASE) * rest + slots % rest
        mine = (slots // rest) % fold == q
        return (mine & (left_col[...] == wanted)).astype(BF16)

    s_pack[:, 0:hidden] = dot(route_pick(), scaled[...], ((0,), (0,))).astype(BF16)
    folded = jnp.zeros((count, part_s), F32)
    for q in range(s_fold):
        folded = folded + dot(
            route_left(q), scaled[:, q * part_s : (q + 1) * part_s], ((0,), (0,))
        )
    s_pack[:, hidden : hidden + part_s] = folded.astype(BF16)

    def scaled_copy(is_far, j):
        g = 1 if is_far else 3
        n = 0 if is_far else 1
        source = s_pack.at[block(j if is_far else half_experts + j)]
        to = (d, (far if is_far else near) + j)
        return remote(source, s.at[block(g * half_experts + at)], tss.at[n], rss.at[n], to)

    def back_copy(is_far, j):
        n = 0 if is_far else 1
        source = c.at[block(j if is_far else half_experts + j)]
        to = (d, (far if is_far else near) + j)
        return remote(source, r.at[block(n * half_experts + at)], tb.at[n], rb.at[n], to)

    def rows_of(g):
        return slice(g * group, (g + 1) * group)

    def rest_of(g):
        return slice(g * rest_group, (g + 1) * rest_group)

    def contract(g, put):
        wait_bytes(x.at[rows_of(g)], rs.at[g])
        for q in range(fold):
            z[rest_of(g), q * part : (q + 1) * part] = dot(
                unfold_pick(half_experts, rest, q), x[rows_of(g), half : half + part], ((1,), (0,))
            ).astype(BF16)
        lhs = jnp.concatenate([x[rows_of(g), 0:half], z[rest_of(g), :]], axis=0)
        for lo in range(0, hidden, 256):
            put(lo, dot(lhs, w[lo : lo + 256, :], ((1,), (1,))))

    across = (other, e)

    def partial_copy(n):
        return remote(px_out.at[n], px_in.at[n], tp.at[n], rp.at[n], across)

    def forward_copy(n):
        g = 1 + 2 * n
        return remote(s.at[rows_of(g)], s.at[rows_of(g - 1)], tf.at[n], rf.at[n], across)

    loads[2].wait()

    def send_partial(n):
        def put(lo, value):
            px_out[n, :, lo : lo + 256] = value.astype(BF16)

        contract(2 * n, put)
        partial_copy(n).start()

    def finish(n):
        def put(lo, value):
            px_out_cut = slice(lo, lo + 256)
            summed = (value + px_in[n, :, px_out_cut].astype(F32)).astype(BF16)
            c[rows_of(n), px_out_cut] = summed[:group]
            c_routes[0:rest_group, px_out_cut] = summed[group:].astype(F32)

        partial_copy(n).wait_recv()
        contract(2 * n + 1, put)
        folded = jnp.zeros((group, part_s), F32)
        for q in range(s_fold):
            folded = folded + dot(
                fold_pick(half_experts, rest, fold, q),
                c_routes[0:rest_group, q * part_s : (q + 1) * part_s].astype(BF16),
                ((1,), (0,)),
            )
        c[rows_of(n), hidden : hidden + part_s] = folded.astype(BF16)

    send_partial(1)
    send_partial(0)

    def start_scaled(k):
        j = (at + k) % half_experts
        scaled_copy(True, j).start()
        scaled_copy(False, j).start()

    scaled_copy(True, at).start()
    loop(1, half_experts, start_scaled)
    pltpu.make_async_copy(
        s_pack.at[block(half_experts + at)], s.at[block(3 * half_experts + at)], rss.at[1]
    ).start()

    finish(1)

    def start_back_near(k):
        back_copy(False, (at + k) % half_experts).start()

    loop(1, half_experts, start_back_near)
    pltpu.make_async_copy(
        c.at[block(half_experts + at)], r.at[block(half_experts + at)], rb.at[1]
    ).start()
    wait_bytes(s.at[rows_of(3)], rss.at[1])
    forward_copy(1).start()

    finish(0)

    def start_back_far(k):
        back_copy(True, (at + k) % half_experts).start()

    loop(0, half_experts, start_back_far)

    def turn(n):
        for g in (2 * n, 2 * n + 1):
            for q in range(s_fold):
                s_rest[rest_of(g), q * part_s : (q + 1) * part_s] = dot(
                    unfold_pick(half_experts, rest, q),
                    s[rows_of(g), hidden : hidden + part_s],
                    ((1,), (0,)),
                ).astype(BF16)
        s_turn[:, 0 : 2 * group] = s[2 * n * group : (2 * n + 2) * group, 0:hidden].T
        s_turn[:, 2 * group : 2 * group + 2 * rest_group] = s_rest[
            2 * n * rest_group : (2 * n + 2) * rest_group, :
        ].T

    def product(n, columns):
        return dot(
            s_turn[:, 0 : 2 * group], x[2 * n * group : (2 * n + 2) * group, columns], ((1,), (0,))
        ) + dot(
            s_turn[:, 2 * group : 2 * group + 2 * rest_group],
            z[2 * n * rest_group : (2 * n + 2) * rest_group, columns],
            ((1,), (0,)),
        )

    forward_copy(1).wait_recv()
    turn(1)

    @pl.loop(0, half // 512)
    def _(j):
        columns = pl.ds(pl.multiple_of(j * 512, 512), 512)
        total[:, columns] = product(1, columns)

    wait_bytes(s.at[rows_of(1)], rss.at[0])
    forward_copy(0).start()
    forward_copy(0).wait_recv()
    turn(0)

    @pl.loop(0, half // 512)
    def _(j):
        columns = pl.ds(pl.multiple_of(j * 512, 512), 512)
        down[:, columns] = (total[:, columns] + product(0, columns)).astype(BF16)

    store_down = pltpu.make_async_copy(down, down_hbm, down_sem)
    store_down.start()

    wait_bytes(r.at[rows_of(1)], rb.at[1])
    wait_bytes(r.at[rows_of(0)], rb.at[0])
    for q in range(s_fold):
        cut = slice(q * part_s, (q + 1) * part_s)
        c_routes[:, cut] = dot(route_pick(), r[:, cut], ((1,), (0,))) + dot(
            route_left(q), r[:, hidden : hidden + part_s], ((1,), (0,))
        )

    @pl.loop(0, tokens // step)
    def _(i):
        mine = pl.ds(pl.multiple_of(i * 2 * step, 2 * step), 2 * step)
        value = c_routes[mine, :]
        gate_col[mine, :] = jnp.sum(plain[mine, :].astype(F32) * value, axis=1, keepdims=True)
        out = jnp.concatenate(
            [value * grad_gate_factor[mine, :], value * grad_up_factor[mine, :]], axis=1
        ).astype(BF16)
        pre_out[pl.ds(pl.multiple_of(i * step, step), step)] = out.reshape(step, 2, 2 * hidden)

    for k in range(2):
        mine = token_of & (first if k == 0 else ~first)
        gate_out[k : k + 1, :] = jnp.sum(
            jnp.where(mine, gate_col[...], 0.0), axis=0, keepdims=True
        ).astype(BF16)

    wait_bytes(pack.at[0, 0:group], ts.at[0])
    wait_bytes(pack.at[1, 0:group], ts.at[1])
    wait_bytes(pack.at[0, group : 2 * group], ts.at[2])
    wait_bytes(pack.at[1, group : 2 * group - BASE], ts.at[3])
    wait_bytes(s_pack.at[0:group], tss.at[0])
    wait_bytes(s_pack.at[group : 2 * group - BASE], tss.at[1])
    wait_bytes(c.at[0:group], tb.at[0])
    wait_bytes(c.at[group : 2 * group - BASE], tb.at[1])
    for n in range(2):
        partial_copy(n).wait_send()
        forward_copy(n).wait_send()
    store_down.wait()


def on_device(grad_out, saved_pre, gate_weight, routes, w_down):
    tokens, top_count = routes.shape
    hidden, half = w_down.shape[1:]
    width = grad_out.shape[1]
    experts = lax.axis_size("expert")
    replicas = lax.axis_size("dp")
    capacity = 5 * tokens * top_count // (4 * experts)
    if (replicas, top_count, experts, capacity, hidden, half % 512) != (2, 2, 16, 20, 768, 0):
        return on_device_general(grad_out, saved_pre, gate_weight, routes, w_down)
    rest = capacity - BASE
    fold = BASE // rest
    s_fold = hidden // 256
    devices = replicas * experts
    count, total = experts * BASE, devices * BASE
    part, part_s = half // fold, hidden // s_fold
    finished = (count + experts * rest) // 2
    vmem = pl.BlockSpec(memory_space=pltpu.VMEM)
    anywhere = pl.BlockSpec(memory_space=pl.ANY)
    dma = pltpu.SemaphoreType.DMA
    pre, gate, down = pl.pallas_call(
        functools.partial(exchange_kernel, experts, rest, fold, s_fold),
        out_shape=(
            jax.ShapeDtypeStruct(saved_pre.shape, BF16),
            jax.ShapeDtypeStruct((top_count, tokens), BF16),
            jax.ShapeDtypeStruct((hidden, half), BF16),
        ),
        in_specs=[vmem, vmem, anywhere, anywhere, anywhere],
        out_specs=[vmem, vmem, anywhere],
        scratch_shapes=[
            pltpu.VMEM((tokens, width), BF16),
            pltpu.VMEM(saved_pre.shape, BF16),
            pltpu.VMEM((hidden, half), BF16),
            pltpu.VMEM((2, count, half + part), BF16),
            pltpu.VMEM((total, half + part), BF16),
            pltpu.VMEM((devices * rest, half), BF16),
            pltpu.VMEM((2 * tokens, hidden), BF16),
            pltpu.VMEM((count, hidden + part_s), BF16),
            pltpu.VMEM((total, hidden + part_s), BF16),
            pltpu.VMEM((devices * rest, hidden), BF16),
            pltpu.VMEM((hidden, finished * 2), BF16),
            pltpu.VMEM((2, finished, hidden), BF16),
            pltpu.VMEM((2, finished, hidden), BF16),
            pltpu.VMEM((count, hidden + part_s), BF16),
            pltpu.VMEM((count, hidden + part_s), BF16),
            pltpu.VMEM((2 * tokens, hidden), F32),
            pltpu.VMEM((2 * tokens, hidden), F32),
            pltpu.VMEM((2 * tokens, hidden), F32),
            pltpu.VMEM((2 * tokens, hidden), BF16),
            pltpu.VMEM((2 * tokens, 1), jnp.int32),
            pltpu.VMEM((2 * tokens, 1), jnp.int32),
            pltpu.VMEM((2 * tokens, 1), F32),
            pltpu.VMEM((2 * tokens, 1), F32),
            pltpu.VMEM((hidden, half), F32),
            pltpu.VMEM((hidden, half), BF16),
            dma((3,)), dma,
            dma((4,)), dma((4,)),
            dma((2,)), dma((2,)), dma((2,)), dma((2,)),
            dma((2,)), dma((2,)), dma((2,)), dma((2,)),
        ],
        compiler_params=pltpu.CompilerParams(
            collective_id=0, has_side_effects=True, vmem_limit_bytes=48 << 20
        ),
    )(routes.T, gate_weight.T, grad_out, saved_pre, w_down[0])
    return pre, gate.T, down[None]


def solution(mesh):
    return jax.shard_map(
        on_device,
        mesh=mesh,
        in_specs=(
            P(("dp", "expert"), None),
            P(("dp", "expert"), None, None),
            P(("dp", "expert"), None),
            P(("dp", "expert"), None),
            P("expert", None, "dp"),
        ),
        out_specs=(
            P(("dp", "expert"), None, None),
            P(("dp", "expert"), None),
            P("expert", None, "dp"),
        ),
        check_vma=False,
    )
```

time: 116 us -> 103 us (0.89)
  Pallas kernels: 101 us -> 95.4 us
  other arithmetic: 4.33 us -> 0 us
  matrix products: 1.44 us -> 0 us
    pallas_call x1, Pallas kernels: 101 us -> 95.4 us  [on_device(): pl.pallas_call(functools.partial(exchange_kernel, experts, rest, fold, s_...]
    slice x2 -> x0, local copies, waits for them, and re-layouts: 4.38 us -> none  [the longest x1 2.72 us: on_device(): saved_pre[:, k]]
    unnamed x4 -> x11, local copies, waits for them, and re-layouts: 3.36 us -> 6.74 us
    convert_element_type x3 -> x0, other arithmetic: 2.34 us -> none  [the longest x2 1.68 us: scaled_hidden(): return (weights.astype(F32)[..., None] * active * up_pre).astype(BF16)]
    dot_general x1 -> x0, matrix products: 1.44 us -> none  [dot(): return lax.dot_general(a, b, (dims, ((), ())), preferred_element_type=F32)]
    reduce_sum x1 -> x0, other arithmetic: 1.21 us -> none  [swiglu_grads(): jnp.sum(plain.astype(F32) * contraction.astype(F32), axis=-1).astype(BF16)]
where the time goes in v1:
time: 103 us
  Pallas kernels  95.4 us (93%)
  local copies, waits for them, and re-layouts  6.74 us (7%)
    pallas_call x1, Pallas kernels, on_device(): pl.pallas_call(functools.partial(exchange_kernel, experts, rest, fold, s_...  95.4 us
    unnamed x11, local copies, waits for them, and re-layouts  6.74 us

profile of v1, /device:TPU:0, one launch (start us, length us, event | category | flops | bytes accessed | tf_op | source)
XLA Modules:
  0.0 102.8 jit_solution(17127830954904977283)
XLA Ops:
  0.6 0.0 copy-start
  0.6 1.2 %copy-done = bf16[128,4096]{1,0:T(8,128)(2,1)S(1)} copy-done((bf16[128,4096]{1,0:T(8,128)(2,1)S(1)}, bf16[128,4096]{1,0:T(8,128)(2,1)}, u32[]{:S(2)}) %copy-start) | copy-done | bytes 1048600
  1.9 0.0 copy-start.1
  1.9 1.1 %copy-done.1 = bf16[128,2,1536]{2,1,0:T(2,128)(2,1)S(1)} copy-done((bf16[128,2,1536]{2,1,0:T(2,128)(2,1)S(1)}, bf16[128,2,1536]{2,1,0:T(2,128)(2,1)}, u32[]{:S(2)}) %copy-start.1) | copy-done | bytes 786456
  3.0 0.0 copy-start.2
  3.0 0.7 copy-done.2
  3.7 0.0 copy-start.3
  3.7 0.7 copy-done.3
  4.3 95.4 %shard_map.76 = (bf16[128,2,1536]{2,1,0:T(2,128)(2,1)S(1)}, bf16[2,128]{1,0:T(2,128)(2,1)S(1)}, bf16[768,2048]{1,0:T(8,128)(2,1)S(1)}) custom-call(s32[2,128]{1,0:T(2,128)S(1)} %bitcast.6, bf16[2,128]{1,0:T(2,128)(2,1)S(1)} %bitcast.7, bf16[128,4096]{1,0:T(8,128)(2,1)S(1)} %copy-done, bf16[128,2,1536]{2,1,0:T(2,128)(2,1)S(1)} %copy-done.1, ...), custom_call_target="tpu_custom_call" | custom-call | tf_op jit(solution)/shard_map/pallas_call | solution.py:485
  99.7 0.9 copy.11
  100.6 0.5 copy.12
  101.1 1.7 %copy.13 = bf16[1,768,2048]{2,1,0:T(8,128)(2,1)} copy(bf16[1,768,2048]{2,1,0:T(8,128)(2,1)S(1)} %bitcast.5) | data formatting | bytes 6291456
Async XLA Ops:
  0.6 1.2 %copy-start = (bf16[128,4096]{1,0:T(8,128)(2,1)S(1)}, bf16[128,4096]{1,0:T(8,128)(2,1)}, u32[]{:S(2)}) copy-start(bf16[128,4096]{1,0:T(8,128)(2,1)} %rows_hbm.1) | copy-start | bytes 3145732
  1.9 1.1 %copy-start.1 = (bf16[128,2,1536]{2,1,0:T(2,128)(2,1)S(1)}, bf16[128,2,1536]{2,1,0:T(2,128)(2,1)}, u32[]{:S(2)}) copy-start(bf16[128,2,1536]{2,1,0:T(2,128)(2,1)} %saved_hbm.1) | copy-start | bytes 2359300
  3.0 0.7 copy-start.2
  3.7 0.7 copy-start.3

commit v2 on v1

--- a/solution.py
+++ b/solution.py
@@ -131,12 +131,13 @@
 
 
 def exchange_kernel(
-    experts, rest, fold, s_fold,
-    routes, weights, rows_hbm, saved_hbm, w_hbm,
-    pre_out, gate_out, down_hbm,
-    rows, saved, w, pack, x, z, scaled, s_pack, s, s_rest, s_turn, px_out, px_in, c, r, c_routes,
-    grad_gate_factor, grad_up_factor, plain, key_col, left_col, weight_col, gate_col, total, down,
-    load_sem, down_sem, ts, rs, tss, rss, tf, rf, tp, rp, tb, rb,
+    experts, rest, fold, s_fold, chunks,
+    routes_hbm, weights_hbm, rows_hbm, saved_hbm, w_hbm,
+    pre_out, gate_out, down,
+    routes, weights, rows, saved, w, pack, raw, names_in, relay_pick, relay, x_far, x, z,
+    scaled, s_pack, s, s_wide, s_rest, s_turn, px_out, px_in, c_wide, c, r, c_routes,
+    grad_gate_factor, grad_up_factor, plain, key_col, left_col, weight_col, gate_col, total,
+    load_sem, tn, rn, tw, rw, tm, rm, tg, rg, tss, rss, tf, rf, tp, rp, tb, rb,
 ):
     d = lax.axis_index("dp")
     e = lax.axis_index("expert")
@@ -146,6 +147,13 @@
     at = e % half_experts
     near = (e // half_experts) * half_experts
     far = half_experts - near
+    quarter = half_experts // 2
+    lane, plane = at % quarter, at // quarter
+    capacity = BASE + rest
+    wide = 2 * capacity
+    slab = relay_pick.shape[1] // half_experts
+    gateway = quarter * (1 + far // half_experts) + lane
+    is_gateway = (e // quarter) % 3 != 0
     tokens, width = rows.shape
     half = width // 2
     part = half // fold
@@ -174,9 +182,13 @@
         lax.fori_loop(first, last, step, 0)
 
     loads = [
-        pltpu.make_async_copy(rows_hbm, rows, load_sem.at[0]),
-        pltpu.make_async_copy(saved_hbm, saved, load_sem.at[1]),
-        pltpu.make_async_copy(w_hbm, w, load_sem.at[2]),
+        pltpu.make_async_copy(source, target, load_sem.at[i])
+        for i, (source, target) in enumerate(
+            (
+                (routes_hbm, routes), (rows_hbm, rows), (weights_hbm, weights), (saved_hbm, saved),
+                (w_hbm, w),
+            )
+        )
     ]
     for load in loads:
         load.start()
@@ -190,53 +202,76 @@
 
     loop(1, 2 * experts, greet)
 
+    loads[0].wait()
     (key0, left0), (key1, left1) = slot_keys(experts, rest, far, routes[...])
-    row = iota((count, tokens), 0)
-    main_pick = ((key0 == row) | (key1 == row)).astype(BF16)
-    slot = (row // BASE) * rest + row % rest
+    row = iota((group, tokens), 0)
+    main_pick = ((key0 == row + group) | (key1 == row + group)).astype(BF16)
+    slot = (row // BASE) * rest + row % rest + rest_group
     hit = (left0 == slot) | (left1 == slot)
     left_pick = jnp.concatenate(
         [(hit & ((row // rest) % fold == q)).astype(BF16) for q in range(fold)], axis=1
     )
 
+    def columns_of(h, lo, size):
+        return pl.ds(pl.multiple_of(h * half + lo, 128), size)
+
     def pack_half(side, h):
-        def columns(lo, size):
-            return pl.ds(pl.multiple_of(h * half + lo, part), size)
-
         for lo in range(0, half, 512):
             pack[side, :, lo : lo + 512] = dot(
-                main_pick, rows[:, columns(lo, 512)], ((1,), (0,))
+                main_pick, rows[:, columns_of(h, lo, 512)], ((1,), (0,))
             ).astype(BF16)
-        folded = jnp.concatenate([rows[:, columns(q * part, part)] for q in range(fold)], axis=0)
+        folded = jnp.concatenate([rows[:, columns_of(h, q * part, part)] for q in range(fold)], axis=0)
         pack[side, :, half : half + part] = dot(left_pick, folded, ((1,), (0,))).astype(BF16)
 
-    def row_copy(side, is_far, j):
-        g = (0 if is_far else 2) + side
-        source = pack.at[side, block(j if is_far else half_experts + j)]
-        to = (other if side == 0 else d, (far if is_far else near) + j)
-        return remote(source, x.at[block(g * half_experts + at)], ts.at[g], rs.at[g], to)
-
-    loads[0].wait()
+    def near_copy(side, j):
+        return remote(
+            pack.at[side, block(j)],
+            x.at[block(side * half_experts + at)],
+            tn.at[side],
+            rn.at[side],
+            (other if side == 0 else d, near + j),
+        )
+
+    chunk, ahead = half // chunks, 3
+
+    def raw_copy(side, n):
+        h = other if side == 0 else d
+        return remote(
+            rows.at[:, columns_of(h, n * chunk, chunk)],
+            raw.at[side, pl.ds(pl.multiple_of(plane * tokens, tokens), tokens), n * chunk : (n + 1) * chunk],
+            tw.at[side * chunks + n],
+            rw.at[side * chunks + n],
+            (h, gateway),
+        )
+
+    def names_copy(side):
+        h = other if side == 0 else d
+        return remote(routes, names_in.at[2 * side + plane], tm.at[0], rm.at[0], (h, gateway))
+
+    loads[1].wait()
     pack_half(0, other)
+    pack_half(1, d)
     pl.semaphore_wait(barrier, 2 * experts - 1)
-
-    def start_across(k):
-        j = (at + k) % half_experts
-        row_copy(0, True, j).start()
-        row_copy(0, False, j).start()
-
-    loop(0, half_experts, start_across)
-    pack_half(1, d)
-
-    def start_own(k):
-        j = (at + k) % half_experts
-        row_copy(1, True, j).start()
-        row_copy(1, False, j).start()
-
-    row_copy(1, True, at).start()
-    loop(1, half_experts, start_own)
+    for side in range(2):
+        names_copy(side).start()
+    for n in range(ahead):
+        for side in range(2):
+            raw_copy(side, n).start()
+
+    def each_near(body):
+        for k in range(quarter):
+            for p in range(2):
+                j = (plane if p == 0 else 1 - plane) * quarter + (lane + k) % quarter
+                body(j, k == 0 and p == 0)
+
+    def start_near(j, is_self):
+        near_copy(0, j).start()
+        if not is_self:
+            near_copy(1, j).start()
+
+    each_near(start_near)
     pltpu.make_async_copy(
-        pack.at[1, block(half_experts + at)], x.at[block(3 * half_experts + at)], rs.at[3]
+        pack.at[1, block(at)], x.at[block(half_experts + at)], rn.at[1]
     ).start()
 
     token_of = iota((2 * tokens, tokens), 0) // 2 == iota((2 * tokens, tokens), 1)
@@ -246,10 +281,11 @@
         value = jnp.where(first, v0.astype(F32), v1.astype(F32))
         return jnp.sum(jnp.where(token_of, value, 0.0), axis=1, keepdims=True)
 
+    loads[2].wait()
     key_col[...] = column(key0, key1).astype(jnp.int32)
     left_col[...] = column(left0, left1).astype(jnp.int32)
     weight_col[...] = column(weights[0:1, :], weights[1:2, :])
-    loads[1].wait()
+    loads[3].wait()
     step = 16
 
     @pl.loop(0, tokens // step)
@@ -303,13 +339,32 @@
     def rest_of(g):
         return slice(g * rest_group, (g + 1) * rest_group)
 
-    def contract(g, put):
-        wait_bytes(x.at[rows_of(g)], rs.at[g])
-        for q in range(fold):
-            z[rest_of(g), q * part : (q + 1) * part] = dot(
-                unfold_pick(half_experts, rest, q), x[rows_of(g), half : half + part], ((1,), (0,))
-            ).astype(BF16)
-        lhs = jnp.concatenate([x[rows_of(g), 0:half], z[rest_of(g), :]], axis=0)
+    def slots_of(side):
+        return slice(side * quarter * wide, (side + 1) * quarter * wide)
+
+    def wide_pick(q, turned):
+        shape = (quarter * wide, group) if turned else (group, quarter * wide)
+        narrow, there = iota(shape, int(turned)), iota(shape, 1 - int(turned))
+        source, inner = narrow // BASE, narrow % BASE
+        base = (source % quarter) * wide + (source // quarter) * capacity
+        if q is None:
+            return (there == base + inner).astype(BF16)
+        return ((there == base + BASE + inner % rest) & (inner // rest == q)).astype(BF16)
+
+    def contract(n, side, put):
+        if n == 0:
+            lanes = slice(side * quarter, (side + 1) * quarter)
+            wait_bytes(x_far.at[lanes], rg.at[side])
+            lhs = x_far[lanes].reshape(quarter * wide, half)
+        else:
+            wait_bytes(x.at[rows_of(side)], rn.at[side])
+            for q in range(fold):
+                z[rest_of(side), q * part : (q + 1) * part] = dot(
+                    unfold_pick(half_experts, rest, q),
+                    x[rows_of(side), half : half + part],
+                    ((1,), (0,)),
+                ).astype(BF16)
+            lhs = jnp.concatenate([x[rows_of(side), 0:half], z[rest_of(side), :]], axis=0)
         for lo in range(0, hidden, 256):
             put(lo, dot(lhs, w[lo : lo + 256, :], ((1,), (1,))))
 
@@ -322,47 +377,114 @@
         g = 1 + 2 * n
         return remote(s.at[rows_of(g)], s.at[rows_of(g - 1)], tf.at[n], rf.at[n], across)
 
-    loads[2].wait()
+    loads[4].wait()
 
     def send_partial(n):
         def put(lo, value):
             px_out[n, :, lo : lo + 256] = value.astype(BF16)
 
-        contract(2 * n, put)
+        contract(n, 0, put)
         partial_copy(n).start()
 
     def finish(n):
         def put(lo, value):
-            px_out_cut = slice(lo, lo + 256)
-            summed = (value + px_in[n, :, px_out_cut].astype(F32)).astype(BF16)
-            c[rows_of(n), px_out_cut] = summed[:group]
-            c_routes[0:rest_group, px_out_cut] = summed[group:].astype(F32)
+            cut = slice(lo, lo + 256)
+            summed = (value + px_in[n, :, cut].astype(F32)).astype(BF16)
+            if n == 0:
+                c_wide[:, cut] = summed
+            else:
+                c[rows_of(n), cut] = summed[:group]
+                c_wide[0:rest_group, cut] = summed[group:]
 
         partial_copy(n).wait_recv()
-        contract(2 * n + 1, put)
+        contract(n, 1, put)
+        if n == 0:
+            c[rows_of(n), 0:hidden] = dot(
+                wide_pick(None, False), c_wide[...], ((1,), (0,))
+            ).astype(BF16)
         folded = jnp.zeros((group, part_s), F32)
         for q in range(s_fold):
-            folded = folded + dot(
-                fold_pick(half_experts, rest, fold, q),
-                c_routes[0:rest_group, q * part_s : (q + 1) * part_s].astype(BF16),
-                ((1,), (0,)),
-            )
+            cut = slice(q * part_s, (q + 1) * part_s)
+            if n == 0:
+                folded = folded + dot(wide_pick(q, False), c_wide[:, cut], ((1,), (0,)))
+            else:
+                folded = folded + dot(
+                    fold_pick(half_experts, rest, fold, q), c_wide[0:rest_group, cut], ((1,), (0,))
+                )
         c[rows_of(n), hidden : hidden + part_s] = folded.astype(BF16)
 
-    send_partial(1)
-    send_partial(0)
-
-    def start_scaled(k):
-        j = (at + k) % half_experts
-        scaled_copy(True, j).start()
-        scaled_copy(False, j).start()
-
-    scaled_copy(True, at).start()
-    loop(1, half_experts, start_scaled)
+    def relay_copy(side, n, j):
+        return remote(
+            relay.at[side, n, j],
+            x_far.at[side * quarter + lane, :, n * chunk : (n + 1) * chunk],
+            tg.at[0],
+            rg.at[side],
+            (d, near + j),
+        )
+
+    def build_relay_pick():
+        wait_bytes(names_in, rm.at[0])
+        before = (iota((tokens, tokens), 0) < iota((tokens, tokens), 1)).astype(BF16)
+        names = iota((half_experts, tokens), 0)
+        target = iota((half_experts * slab, tokens), 0)
+        for side in range(2):
+            for p in range(2):
+                named = [names_in[2 * side + p, k : k + 1, :] - near for k in range(2)]
+                onehot = [(named[k] == names).astype(F32) for k in range(2)]
+                counts = dot((onehot[0] + onehot[1]).astype(BF16), before, ((1,), (0,)))
+                hits = []
+                for k in range(2):
+                    rank = jnp.sum(counts * onehot[k], axis=0, keepdims=True).astype(jnp.int32)
+                    here = (named[k] >= 0) & (named[k] < half_experts)
+                    hits.append(target == jnp.where(here, named[k] * slab + p * capacity + rank, -1))
+                relay_pick[side, :, p * tokens : (p + 1) * tokens] = (hits[0] | hits[1]).astype(BF16)
+
+    def relay_step(side, n):
+        cut = slice(n * chunk, (n + 1) * chunk)
+        wait_bytes(raw.at[side, :, cut], rw.at[side * chunks + n])
+        packed = dot(relay_pick[side], raw[side, :, cut], ((1,), (0,))).astype(BF16)
+        for j in range(half_experts):
+            relay[side, n, j] = packed[j * slab : j * slab + wide]
+
+        def start(j, is_self):
+            if not is_self:
+                relay_copy(side, n, j).start()
+
+        each_near(start)
+        pltpu.make_async_copy(
+            relay.at[side, n, at],
+            x_far.at[side * quarter + lane, :, cut],
+            rg.at[side],
+        ).start()
+
+    def raw_steps(first, last):
+        for n in range(first, last):
+
+            @pl.when(is_gateway)
+            def _():
+                for side in range(2):
+                    relay_step(side, n)
+
+            for side in range(2):
+                raw_copy(side, n).wait_send()
+                if n + ahead < chunks:
+                    raw_copy(side, n + ahead).start()
+
+    def scaled_start(is_far):
+        def start(k):
+            scaled_copy(is_far, (at + k) % half_experts).start()
+
+        loop(0 if is_far else 1, half_experts, start)
+
+    pl.when(is_gateway)(build_relay_pick)
+    raw_steps(0, chunks // 4)
+    scaled_start(False)
     pltpu.make_async_copy(
         s_pack.at[block(half_experts + at)], s.at[block(3 * half_experts + at)], rss.at[1]
     ).start()
-
+    raw_steps(chunks // 4, chunks // 2)
+    send_partial(1)
+    raw_steps(chunks // 2, 3 * chunks // 4)
     finish(1)
 
     def start_back_near(k):
@@ -375,6 +497,9 @@
     wait_bytes(s.at[rows_of(3)], rss.at[1])
     forward_copy(1).start()
 
+    raw_steps(3 * chunks // 4, chunks)
+    scaled_start(True)
+    send_partial(0)
     finish(0)
 
     def start_back_far(k):
@@ -383,25 +508,32 @@
     loop(0, half_experts, start_back_far)
 
     def turn(n):
-        for g in (2 * n, 2 * n + 1):
+        for side in range(2):
+            g = 2 * n + side
             for q in range(s_fold):
-                s_rest[rest_of(g), q * part_s : (q + 1) * part_s] = dot(
-                    unfold_pick(half_experts, rest, q),
-                    s[rows_of(g), hidden : hidden + part_s],
-                    ((1,), (0,)),
-                ).astype(BF16)
-        s_turn[:, 0 : 2 * group] = s[2 * n * group : (2 * n + 2) * group, 0:hidden].T
-        s_turn[:, 2 * group : 2 * group + 2 * rest_group] = s_rest[
-            2 * n * rest_group : (2 * n + 2) * rest_group, :
-        ].T
+                cut = slice(q * part_s, (q + 1) * part_s)
+                tail = s[rows_of(g), hidden : hidden + part_s]
+                if n == 0:
+                    s_wide[slots_of(side), cut] = (
+                        dot(wide_pick(None, True), s[rows_of(g), cut], ((1,), (0,)))
+                        + dot(wide_pick(q, True), tail, ((1,), (0,)))
+                    ).astype(BF16)
+                else:
+                    s_rest[rest_of(side), cut] = dot(
+                        unfold_pick(half_experts, rest, q), tail, ((1,), (0,))
+                    ).astype(BF16)
+        if n == 0:
+            s_turn[...] = s_wide[...].T
+        else:
+            s_turn[:, 0 : 2 * group] = s[2 * group : 4 * group, 0:hidden].T
+            s_turn[:, 2 * group : 2 * group + 2 * rest_group] = s_rest[...].T
 
     def product(n, columns):
-        return dot(
-            s_turn[:, 0 : 2 * group], x[2 * n * group : (2 * n + 2) * group, columns], ((1,), (0,))
-        ) + dot(
-            s_turn[:, 2 * group : 2 * group + 2 * rest_group],
-            z[2 * n * rest_group : (2 * n + 2) * rest_group, columns],
-            ((1,), (0,)),
+        if n == 0:
+            rhs = x_far[:, :, columns].reshape(2 * quarter * wide, columns.size)
+            return dot(s_turn[...], rhs, ((1,), (0,)))
+        return dot(s_turn[:, 0 : 2 * group], x[:, columns], ((1,), (0,))) + dot(
+            s_turn[:, 2 * group : 2 * group + 2 * rest_group], z[:, columns], ((1,), (0,))
         )
 
     forward_copy(1).wait_recv()
@@ -421,9 +553,6 @@
     def _(j):
         columns = pl.ds(pl.multiple_of(j * 512, 512), 512)
         down[:, columns] = (total[:, columns] + product(0, columns)).astype(BF16)
-
-    store_down = pltpu.make_async_copy(down, down_hbm, down_sem)
-    store_down.start()
 
     wait_bytes(r.at[rows_of(1)], rb.at[1])
     wait_bytes(r.at[rows_of(0)], rb.at[0])
@@ -449,10 +578,14 @@
             jnp.where(mine, gate_col[...], 0.0), axis=0, keepdims=True
         ).astype(BF16)
 
-    wait_bytes(pack.at[0, 0:group], ts.at[0])
-    wait_bytes(pack.at[1, 0:group], ts.at[1])
-    wait_bytes(pack.at[0, group : 2 * group], ts.at[2])
-    wait_bytes(pack.at[1, group : 2 * group - BASE], ts.at[3])
+    wait_bytes(pack.at[0], tn.at[0])
+    wait_bytes(pack.at[1, 0 : group - BASE], tn.at[1])
+    wait_bytes(names_in.at[0:2], tm.at[0])
+
+    @pl.when(is_gateway)
+    def _():
+        wait_bytes(relay.at[:, :, 0 : half_experts - 1], tg.at[0])
+
     wait_bytes(s_pack.at[0:group], tss.at[0])
     wait_bytes(s_pack.at[group : 2 * group - BASE], tss.at[1])
     wait_bytes(c.at[0:group], tb.at[0])
@@ -460,7 +593,14 @@
     for n in range(2):
         partial_copy(n).wait_send()
         forward_copy(n).wait_send()
-    store_down.wait()
+
+
+def store_kernel(*refs):
+    copies = [pltpu.make_async_copy(refs[i], refs[3 + i], refs[6].at[i]) for i in range(3)]
+    for copy in copies:
+        copy.start()
+    for copy in copies:
+        copy.wait()
 
 
 def on_device(grad_out, saved_pre, gate_weight, routes, w_down):
@@ -479,32 +619,42 @@
     count, total = experts * BASE, devices * BASE
     part, part_s = half // fold, hidden // s_fold
     finished = (count + experts * rest) // 2
+    chunks = half // 256
     vmem = pl.BlockSpec(memory_space=pltpu.VMEM)
-    anywhere = pl.BlockSpec(memory_space=pl.ANY)
+    stored = pl.BlockSpec(memory_space=pltpu.HBM)
     dma = pltpu.SemaphoreType.DMA
     pre, gate, down = pl.pallas_call(
-        functools.partial(exchange_kernel, experts, rest, fold, s_fold),
+        functools.partial(exchange_kernel, experts, rest, fold, s_fold, chunks),
         out_shape=(
-            jax.ShapeDtypeStruct(saved_pre.shape, BF16),
-            jax.ShapeDtypeStruct((top_count, tokens), BF16),
-            jax.ShapeDtypeStruct((hidden, half), BF16),
+            pltpu.VMEM(saved_pre.shape, BF16),
+            pltpu.VMEM((top_count, tokens), BF16),
+            pltpu.VMEM((hidden, half), BF16),
         ),
-        in_specs=[vmem, vmem, anywhere, anywhere, anywhere],
-        out_specs=[vmem, vmem, anywhere],
+        in_specs=[stored] * 5,
+        out_specs=[vmem] * 3,
         scratch_shapes=[
+            pltpu.VMEM((top_count, tokens), jnp.int32),
+            pltpu.VMEM((top_count, tokens), BF16),
             pltpu.VMEM((tokens, width), BF16),
             pltpu.VMEM(saved_pre.shape, BF16),
             pltpu.VMEM((hidden, half), BF16),
-            pltpu.VMEM((2, count, half + part), BF16),
-            pltpu.VMEM((total, half + part), BF16),
-            pltpu.VMEM((devices * rest, half), BF16),
+            pltpu.VMEM((2, count // 2, half + part), BF16),
+            pltpu.VMEM((2, 2 * tokens, half), BF16),
+            pltpu.VMEM((4, top_count, tokens), jnp.int32),
+            pltpu.VMEM((2, experts // 2 * -(-2 * capacity // 16) * 16, 2 * tokens), BF16),
+            pltpu.VMEM((2, chunks, experts // 2, 2 * capacity, half // chunks), BF16),
+            pltpu.VMEM((experts // 2, 2 * capacity, half), BF16),
+            pltpu.VMEM((count, half + part), BF16),
+            pltpu.VMEM((experts * rest, half), BF16),
             pltpu.VMEM((2 * tokens, hidden), BF16),
             pltpu.VMEM((count, hidden + part_s), BF16),
             pltpu.VMEM((total, hidden + part_s), BF16),
-            pltpu.VMEM((devices * rest, hidden), BF16),
-            pltpu.VMEM((hidden, finished * 2), BF16),
+            pltpu.VMEM((2 * finished, hidden), BF16),
+            pltpu.VMEM((experts * rest, hidden), BF16),
+            pltpu.VMEM((hidden, 2 * finished), BF16),
             pltpu.VMEM((2, finished, hidden), BF16),
             pltpu.VMEM((2, finished, hidden), BF16),
+            pltpu.VMEM((finished, hidden), BF16),
             pltpu.VMEM((count, hidden + part_s), BF16),
             pltpu.VMEM((count, hidden + part_s), BF16),
             pltpu.VMEM((2 * tokens, hidden), F32),
@@ -516,16 +666,27 @@
             pltpu.VMEM((2 * tokens, 1), F32),
             pltpu.VMEM((2 * tokens, 1), F32),
             pltpu.VMEM((hidden, half), F32),
-            pltpu.VMEM((hidden, half), BF16),
-            dma((3,)), dma,
-            dma((4,)), dma((4,)),
+            dma((5,)),
+            dma((2,)), dma((2,)), dma((2 * chunks,)), dma((2 * chunks,)), dma((1,)), dma((1,)),
+            dma((1,)), dma((2,)),
             dma((2,)), dma((2,)), dma((2,)), dma((2,)),
             dma((2,)), dma((2,)), dma((2,)), dma((2,)),
         ],
         compiler_params=pltpu.CompilerParams(
-            collective_id=0, has_side_effects=True, vmem_limit_bytes=48 << 20
+            collective_id=0, has_side_effects=True, vmem_limit_bytes=40 << 20
         ),
-    )(routes.T, gate_weight.T, grad_out, saved_pre, w_down[0])
+    )(*[
+        pltpu.with_memory_space_constraint(operand, pltpu.HBM)
+        for operand in (routes.T, gate_weight.T, grad_out, saved_pre, w_down[0])
+    ])
+    pre, gate, down = pl.pallas_call(
+        store_kernel,
+        out_shape=[jax.ShapeDtypeStruct(a.shape, a.dtype) for a in (pre, gate, down)],
+        in_specs=[vmem] * 3,
+        out_specs=[stored] * 3,
+        scratch_shapes=[dma((3,))],
+        compiler_params=pltpu.CompilerParams(vmem_limit_bytes=1 << 20),
+    )(pre, gate, down)
     return pre, gate.T, down[None]
 
 

time: 103 us -> 94.2 us (0.915)
  local copies, waits for them, and re-layouts: 6.74 us -> 0 us
  Pallas kernels: 95.4 us -> 93.3 us
    unnamed x11 -> x0, local copies, waits for them, and re-layouts: 6.74 us -> none
    pallas_call x1, Pallas kernels: 95.4 us -> 91.3 us  [on_device(): pl.pallas_call(functools.partial(exchange_kernel, experts, rest, fold, s_...]
    pallas_call x0 -> x1, Pallas kernels: none -> 1.96 us  [on_device(): pl.pallas_call(store_kernel, out_shape=[jax.ShapeDtypeStruct(a.shape, a.d...]
where the time goes in v2:
time: 94.2 us; the launch traced here: 93.9 us
  Pallas kernels  93.3 us (99%)
    pallas_call x1, Pallas kernels, on_device(): pl.pallas_call(functools.partial(exchange_kernel, experts, rest, fold, s_...  91.3 us
    pallas_call x1, Pallas kernels, on_device(): pl.pallas_call(store_kernel, out_shape=[jax.ShapeDtypeStruct(a.shape, a.d...  1.96 us

profile of v2, /device:TPU:0, one launch (start us, length us, event | category | flops | bytes accessed | tf_op | source)
XLA Modules:
  0.0 93.9 jit_solution(8733238486548769540)
XLA Ops:
  0.6 91.3 %shard_map.76 = (bf16[128,2,1536]{2,1,0:T(2,128)(2,1)S(1)}, bf16[2,128]{1,0:T(2,128)(2,1)S(1)}, bf16[768,2048]{1,0:T(8,128)(2,1)S(1)}) custom-call(s32[2,128]{1,0:T(2,128)} %bitcast.6, bf16[2,128]{1,0:T(2,128)(2,1)} %bitcast.7, bf16[128,4096]{1,0:T(8,128)(2,1)} %rows_hbm.1, bf16[128,2,1536]{2,1,0:T(2,128)(2,1)} %saved_hbm.1, bf16[768,2048]{1,0:T(8,128)(2,1)} %bitcast.5), custom_call_target="tpu_custom_call" | custom-call | tf_op jit(solution)/shard_map/pallas_call | solution.py:626
  92.0 2.0 %shard_map.77 = (bf16[128,2,1536]{2,1,0:T(2,128)(2,1)}, bf16[2,128]{1,0:T(2,128)(2,1)}, bf16[768,2048]{1,0:T(8,128)(2,1)}) custom-call(bf16[128,2,1536]{2,1,0:T(2,128)(2,1)S(1)} %get-tuple-element.9.refs_0_, bf16[2,128]{1,0:T(2,128)(2,1)S(1)} %get-tuple-element.10.refs_1_, bf16[768,2048]{1,0:T(8,128)(2,1)S(1)} %get-tuple-element.11.refs_2_), custom_call_target="tpu_custom_call" | custom-call | tf_op jit(solution)/shard_map/pallas_call | solution.py:682

commit v3 on v2

--- a/solution.py
+++ b/solution.py
@@ -135,7 +135,7 @@
     routes_hbm, weights_hbm, rows_hbm, saved_hbm, w_hbm,
     pre_out, gate_out, down,
     routes, weights, rows, saved, w, pack, raw, names_in, relay_pick, relay, x_far, x, z,
-    scaled, s_pack, s, s_wide, s_rest, s_turn, px_out, px_in, c_wide, c, r, c_routes,
+    scaled, s_pack, s, s_wide, s_rest, s_turn, s_far, px_out, px_in, c_wide, c, r, c_routes,
     grad_gate_factor, grad_up_factor, plain, key_col, left_col, weight_col, gate_col, total,
     load_sem, tn, rn, tw, rw, tm, rm, tg, rg, tss, rss, tf, rf, tp, rp, tb, rb,
 ):
@@ -232,7 +232,10 @@
             (other if side == 0 else d, near + j),
         )
 
-    chunk, ahead = half // chunks, 3
+    chunk, ahead, lead = half // chunks, 8, 3
+    order = [(0, n) for n in range(lead)]
+    for n in range(chunks):
+        order += [(0, n + lead)] * (n + lead < chunks) + [(1, n)]
 
     def raw_copy(side, n):
         h = other if side == 0 else d
@@ -254,9 +257,8 @@
     pl.semaphore_wait(barrier, 2 * experts - 1)
     for side in range(2):
         names_copy(side).start()
-    for n in range(ahead):
-        for side in range(2):
-            raw_copy(side, n).start()
+    for side, n in order[:ahead]:
+        raw_copy(side, n).start()
 
     def each_near(body):
         for k in range(quarter):
@@ -264,12 +266,14 @@
                 j = (plane if p == 0 else 1 - plane) * quarter + (lane + k) % quarter
                 body(j, k == 0 and p == 0)
 
-    def start_near(j, is_self):
-        near_copy(0, j).start()
+    def start_near_own(j, is_self):
         if not is_self:
             near_copy(1, j).start()
 
-    each_near(start_near)
+    def start_near_across(j, is_self):
+        near_copy(0, j).start()
+
+    each_near(start_near_own)
     pltpu.make_async_copy(
         pack.at[1, block(at)], x.at[block(half_experts + at)], rn.at[1]
     ).start()
@@ -322,10 +326,10 @@
 
     def scaled_copy(is_far, j):
         g = 1 if is_far else 3
-        n = 0 if is_far else 1
+        n = 1 + at if is_far else 0
         source = s_pack.at[block(j if is_far else half_experts + j)]
         to = (d, (far if is_far else near) + j)
-        return remote(source, s.at[block(g * half_experts + at)], tss.at[n], rss.at[n], to)
+        return remote(source, s.at[block(g * half_experts + at)], tss.at[int(is_far)], rss.at[n], to)
 
     def back_copy(is_far, j):
         n = 0 if is_far else 1
@@ -373,9 +377,13 @@
     def partial_copy(n):
         return remote(px_out.at[n], px_in.at[n], tp.at[n], rp.at[n], across)
 
-    def forward_copy(n):
-        g = 1 + 2 * n
-        return remote(s.at[rows_of(g)], s.at[rows_of(g - 1)], tf.at[n], rf.at[n], across)
+    def forward_near():
+        return remote(s.at[rows_of(3)], s.at[rows_of(2)], tf.at[0], rf.at[0], across)
+
+    def forward_far(j):
+        return remote(
+            s.at[block(half_experts + j)], s.at[block(j)], tf.at[1 + j], rf.at[1 + j], across
+        )
 
     loads[4].wait()
 
@@ -458,17 +466,15 @@
         ).start()
 
     def raw_steps(first, last):
-        for n in range(first, last):
+        for i in range(first, last):
 
             @pl.when(is_gateway)
             def _():
-                for side in range(2):
-                    relay_step(side, n)
-
-            for side in range(2):
-                raw_copy(side, n).wait_send()
-                if n + ahead < chunks:
-                    raw_copy(side, n + ahead).start()
+                relay_step(*order[i])
+
+            raw_copy(*order[i]).wait_send()
+            if i + ahead < len(order):
+                raw_copy(*order[i + ahead]).start()
 
     def scaled_start(is_far):
         def start(k):
@@ -477,16 +483,27 @@
         loop(0 if is_far else 1, half_experts, start)
 
     pl.when(is_gateway)(build_relay_pick)
-    raw_steps(0, chunks // 4)
+    each_near(start_near_across)
+    raw_steps(0, 4)
     scaled_start(False)
     pltpu.make_async_copy(
-        s_pack.at[block(half_experts + at)], s.at[block(3 * half_experts + at)], rss.at[1]
+        s_pack.at[block(half_experts + at)], s.at[block(3 * half_experts + at)], rss.at[0]
     ).start()
-    raw_steps(chunks // 4, chunks // 2)
+    raw_steps(4, 10)
+    wait_bytes(s.at[rows_of(3)], rss.at[0])
+    forward_near().start()
     send_partial(1)
-    raw_steps(chunks // 2, 3 * chunks // 4)
+    raw_steps(10, 14)
+    send_partial(0)
+    raw_steps(14, 16)
+    scaled_start(True)
+    finish(0)
+    def start_back_far(k):
+        back_copy(True, (at + k) % half_experts).start()
+
+    loop(0, half_experts, start_back_far)
+
     finish(1)
-
     def start_back_near(k):
         back_copy(False, (at + k) % half_experts).start()
 
@@ -494,65 +511,70 @@
     pltpu.make_async_copy(
         c.at[block(half_experts + at)], r.at[block(half_experts + at)], rb.at[1]
     ).start()
-    wait_bytes(s.at[rows_of(3)], rss.at[1])
-    forward_copy(1).start()
-
-    raw_steps(3 * chunks // 4, chunks)
-    scaled_start(True)
-    send_partial(0)
-    finish(0)
-
-    def start_back_far(k):
-        back_copy(True, (at + k) % half_experts).start()
-
-    loop(0, half_experts, start_back_far)
-
-    def turn(n):
+
+
+    def widen(side):
+        for q in range(s_fold):
+            cut = slice(q * part_s, (q + 1) * part_s)
+            s_wide[slots_of(side), cut] = (
+                dot(wide_pick(None, True), s[rows_of(side), cut], ((1,), (0,)))
+                + dot(wide_pick(q, True), s[rows_of(side), hidden : hidden + part_s], ((1,), (0,)))
+            ).astype(BF16)
+
+    def turn_near():
         for side in range(2):
-            g = 2 * n + side
             for q in range(s_fold):
-                cut = slice(q * part_s, (q + 1) * part_s)
-                tail = s[rows_of(g), hidden : hidden + part_s]
-                if n == 0:
-                    s_wide[slots_of(side), cut] = (
-                        dot(wide_pick(None, True), s[rows_of(g), cut], ((1,), (0,)))
-                        + dot(wide_pick(q, True), tail, ((1,), (0,)))
-                    ).astype(BF16)
-                else:
-                    s_rest[rest_of(side), cut] = dot(
-                        unfold_pick(half_experts, rest, q), tail, ((1,), (0,))
-                    ).astype(BF16)
-        if n == 0:
-            s_turn[...] = s_wide[...].T
-        else:
-            s_turn[:, 0 : 2 * group] = s[2 * group : 4 * group, 0:hidden].T
-            s_turn[:, 2 * group : 2 * group + 2 * rest_group] = s_rest[...].T
-
-    def product(n, columns):
-        if n == 0:
-            rhs = x_far[:, :, columns].reshape(2 * quarter * wide, columns.size)
-            return dot(s_turn[...], rhs, ((1,), (0,)))
+                s_rest[rest_of(side), q * part_s : (q + 1) * part_s] = dot(
+                    unfold_pick(half_experts, rest, q),
+                    s[rows_of(2 + side), hidden : hidden + part_s],
+                    ((1,), (0,)),
+                ).astype(BF16)
+        s_turn[:, 0 : 2 * group] = s[2 * group : 4 * group, 0:hidden].T
+        s_turn[:, 2 * group : 2 * group + 2 * rest_group] = s_rest[...].T
+
+    def near_product(columns):
         return dot(s_turn[:, 0 : 2 * group], x[:, columns], ((1,), (0,))) + dot(
             s_turn[:, 2 * group : 2 * group + 2 * rest_group], z[:, columns], ((1,), (0,))
         )
 
-    forward_copy(1).wait_recv()
-    turn(1)
-
-    @pl.loop(0, half // 512)
-    def _(j):
-        columns = pl.ds(pl.multiple_of(j * 512, 512), 512)
-        total[:, columns] = product(1, columns)
-
-    wait_bytes(s.at[rows_of(1)], rss.at[0])
-    forward_copy(0).start()
-    forward_copy(0).wait_recv()
-    turn(0)
-
-    @pl.loop(0, half // 512)
-    def _(j):
-        columns = pl.ds(pl.multiple_of(j * 512, 512), 512)
-        down[:, columns] = (total[:, columns] + product(0, columns)).astype(BF16)
+    def far_product(side, columns):
+        rhs = x_far[side * quarter : (side + 1) * quarter, :, columns]
+        return dot(s_far[side], rhs.reshape(quarter * wide, columns.size), ((1,), (0,)))
+
+    def each_columns(body):
+        @pl.loop(0, half // 512)
+        def _(j):
+            body(pl.ds(pl.multiple_of(j * 512, 512), 512))
+
+    forward_near().wait_recv()
+    turn_near()
+
+    def add_near(columns):
+        total[:, columns] = near_product(columns)
+
+    each_columns(add_near)
+
+    def pass_on(k):
+        j = (at + half_experts - k) % half_experts
+        wait_bytes(s.at[block(half_experts + j)], rss.at[1 + j])
+        forward_far(j).start()
+
+    loop(0, half_experts, pass_on)
+    widen(1)
+    s_far[1] = s_wide[slots_of(1), :].T
+
+    def add_own(columns):
+        total[:, columns] = total[:, columns] + far_product(1, columns)
+
+    each_columns(add_own)
+    loop(0, half_experts, lambda j: forward_far(j).wait_recv())
+    widen(0)
+    s_far[0] = s_wide[slots_of(0), :].T
+
+    def add_across(columns):
+        down[:, columns] = (total[:, columns] + far_product(0, columns)).astype(BF16)
+
+    each_columns(add_across)
 
     wait_bytes(r.at[rows_of(1)], rb.at[1])
     wait_bytes(r.at[rows_of(0)], rb.at[0])
@@ -586,13 +608,14 @@
     def _():
         wait_bytes(relay.at[:, :, 0 : half_experts - 1], tg.at[0])
 
-    wait_bytes(s_pack.at[0:group], tss.at[0])
-    wait_bytes(s_pack.at[group : 2 * group - BASE], tss.at[1])
+    wait_bytes(s_pack.at[0:group], tss.at[1])
+    wait_bytes(s_pack.at[group : 2 * group - BASE], tss.at[0])
     wait_bytes(c.at[0:group], tb.at[0])
     wait_bytes(c.at[group : 2 * group - BASE], tb.at[1])
     for n in range(2):
         partial_copy(n).wait_send()
-        forward_copy(n).wait_send()
+    forward_near().wait_send()
+    loop(0, half_experts, lambda j: forward_far(j).wait_send())
 
 
 def store_kernel(*refs):
@@ -652,6 +675,7 @@
             pltpu.VMEM((2 * finished, hidden), BF16),
             pltpu.VMEM((experts * rest, hidden), BF16),
             pltpu.VMEM((hidden, 2 * finished), BF16),
+            pltpu.VMEM((2, hidden, finished), BF16),
             pltpu.VMEM((2, finished, hidden), BF16),
             pltpu.VMEM((2, finished, hidden), BF16),
             pltpu.VMEM((finished, hidden), BF16),
@@ -669,7 +693,7 @@
             dma((5,)),
             dma((2,)), dma((2,)), dma((2 * chunks,)), dma((2 * chunks,)), dma((1,)), dma((1,)),
             dma((1,)), dma((2,)),
-            dma((2,)), dma((2,)), dma((2,)), dma((2,)),
+            dma((2,)), dma((experts,)), dma((experts,)), dma((experts,)),
             dma((2,)), dma((2,)), dma((2,)), dma((2,)),
         ],
         compiler_params=pltpu.CompilerParams(

time: 94.2 us -> 88.5 us (0.939)
  Pallas kernels: 93.3 us -> 87.7 us
    pallas_call x1, Pallas kernels: 91.3 us -> 85.8 us  [on_device(): pl.pallas_call(functools.partial(exchange_kernel, experts, rest, fold, s_...]
where the time goes in v3:
time: 88.5 us; the launch traced here: 88.4 us
  Pallas kernels  87.7 us (99%)
    pallas_call x1, Pallas kernels, on_device(): pl.pallas_call(functools.partial(exchange_kernel, experts, rest, fold, s_...  85.8 us
    pallas_call x1, Pallas kernels, on_device(): pl.pallas_call(store_kernel, out_shape=[jax.ShapeDtypeStruct(a.shape, a.d...  1.96 us

profile of v3, /device:TPU:0, one launch (start us, length us, event | category | flops | bytes accessed | tf_op | source)
XLA Modules:
  0.0 88.4 jit_solution(17621626914123313242)
XLA Ops:
  0.6 85.8 %shard_map.76 = (bf16[128,2,1536]{2,1,0:T(2,128)(2,1)S(1)}, bf16[2,128]{1,0:T(2,128)(2,1)S(1)}, bf16[768,2048]{1,0:T(8,128)(2,1)S(1)}) custom-call(s32[2,128]{1,0:T(2,128)} %bitcast.6, bf16[2,128]{1,0:T(2,128)(2,1)} %bitcast.7, bf16[128,4096]{1,0:T(8,128)(2,1)} %rows_hbm.1, bf16[128,2,1536]{2,1,0:T(2,128)(2,1)} %saved_hbm.1, bf16[768,2048]{1,0:T(8,128)(2,1)} %bitcast.5), custom_call_target="tpu_custom_call" | custom-call | tf_op jit(solution)/shard_map/pallas_call | solution.py:649
  86.4 2.0 %shard_map.77 = (bf16[128,2,1536]{2,1,0:T(2,128)(2,1)}, bf16[2,128]{1,0:T(2,128)(2,1)}, bf16[768,2048]{1,0:T(8,128)(2,1)}) custom-call(bf16[128,2,1536]{2,1,0:T(2,128)(2,1)S(1)} %get-tuple-element.9.refs_0_, bf16[2,128]{1,0:T(2,128)(2,1)S(1)} %get-tuple-element.10.refs_1_, bf16[768,2048]{1,0:T(8,128)(2,1)S(1)} %get-tuple-element.11.refs_2_), custom_call_target="tpu_custom_call" | custom-call | tf_op jit(solution)/shard_map/pallas_call | solution.py:706

commit v4 on v3

--- a/solution.py
+++ b/solution.py
@@ -135,7 +135,7 @@
     routes_hbm, weights_hbm, rows_hbm, saved_hbm, w_hbm,
     pre_out, gate_out, down,
     routes, weights, rows, saved, w, pack, raw, names_in, relay_pick, relay, x_far, x, z,
-    scaled, s_pack, s, s_wide, s_rest, s_turn, s_far, px_out, px_in, c_wide, c, r, c_routes,
+    scaled, s_pack, s, s_wide, s_rest, s_turn, s_far, px_out, px_in, c_wide, c, r, c_routes, picks,
     grad_gate_factor, grad_up_factor, plain, key_col, left_col, weight_col, gate_col, total,
     load_sem, tn, rn, tw, rw, tm, rm, tg, rg, tss, rss, tf, rf, tp, rp, tb, rb,
 ):
@@ -232,7 +232,7 @@
             (other if side == 0 else d, near + j),
         )
 
-    chunk, ahead, lead = half // chunks, 8, 3
+    chunk, ahead, lead = half // chunks, 8, 5
     order = [(0, n) for n in range(lead)]
     for n in range(chunks):
         order += [(0, n + lead)] * (n + lead < chunks) + [(1, n)]
@@ -308,19 +308,17 @@
 
     slots = iota((2 * tokens, count), 1)
 
-    def route_pick():
-        return (key_col[...] == slots).astype(BF16)
-
-    def route_left(q):
-        wanted = (slots // BASE) * rest + slots % rest
-        mine = (slots // rest) % fold == q
-        return (mine & (left_col[...] == wanted)).astype(BF16)
-
-    s_pack[:, 0:hidden] = dot(route_pick(), scaled[...], ((0,), (0,))).astype(BF16)
+    picks[0] = (key_col[...] == slots).astype(BF16)
+    wanted = (slots // BASE) * rest + slots % rest
+    hit = left_col[...] == wanted
+    for q in range(s_fold):
+        picks[1 + q] = (hit & ((slots // rest) % fold == q)).astype(BF16)
+
+    s_pack[:, 0:hidden] = dot(picks[0], scaled[...], ((0,), (0,))).astype(BF16)
     folded = jnp.zeros((count, part_s), F32)
     for q in range(s_fold):
         folded = folded + dot(
-            route_left(q), scaled[:, q * part_s : (q + 1) * part_s], ((0,), (0,))
+            picks[1 + q], scaled[:, q * part_s : (q + 1) * part_s], ((0,), (0,))
         )
     s_pack[:, hidden : hidden + part_s] = folded.astype(BF16)
 
@@ -483,17 +481,17 @@
         loop(0 if is_far else 1, half_experts, start)
 
     pl.when(is_gateway)(build_relay_pick)
-    each_near(start_near_across)
-    raw_steps(0, 4)
     scaled_start(False)
     pltpu.make_async_copy(
         s_pack.at[block(half_experts + at)], s.at[block(3 * half_experts + at)], rss.at[0]
     ).start()
-    raw_steps(4, 10)
+    raw_steps(0, 4)
+    each_near(start_near_across)
+    raw_steps(4, 8)
     wait_bytes(s.at[rows_of(3)], rss.at[0])
     forward_near().start()
+    raw_steps(8, 14)
     send_partial(1)
-    raw_steps(10, 14)
     send_partial(0)
     raw_steps(14, 16)
     scaled_start(True)
@@ -576,13 +574,19 @@
 
     each_columns(add_across)
 
+    def unpermuted(n, q):
+        cut = slice(q * part_s, (q + 1) * part_s)
+        return dot(picks[0, :, rows_of(n)], r[rows_of(n), cut], ((1,), (0,))) + dot(
+            picks[1 + q, :, rows_of(n)], r[rows_of(n), hidden : hidden + part_s], ((1,), (0,))
+        )
+
     wait_bytes(r.at[rows_of(1)], rb.at[1])
+    for q in range(s_fold):
+        c_routes[:, q * part_s : (q + 1) * part_s] = unpermuted(1, q)
     wait_bytes(r.at[rows_of(0)], rb.at[0])
     for q in range(s_fold):
         cut = slice(q * part_s, (q + 1) * part_s)
-        c_routes[:, cut] = dot(route_pick(), r[:, cut], ((1,), (0,))) + dot(
-            route_left(q), r[:, hidden : hidden + part_s], ((1,), (0,))
-        )
+        c_routes[:, cut] = c_routes[:, cut] + unpermuted(0, q)
 
     @pl.loop(0, tokens // step)
     def _(i):
@@ -682,6 +686,7 @@
             pltpu.VMEM((count, hidden + part_s), BF16),
             pltpu.VMEM((count, hidden + part_s), BF16),
             pltpu.VMEM((2 * tokens, hidden), F32),
+            pltpu.VMEM((1 + s_fold, 2 * tokens, count), BF16),
             pltpu.VMEM((2 * tokens, hidden), F32),
             pltpu.VMEM((2 * tokens, hidden), F32),
             pltpu.VMEM((2 * tokens, hidden), BF16),

time: 88.5 us -> 85.3 us (0.964)
  Pallas kernels: 87.7 us -> 84.5 us
    pallas_call x1, Pallas kernels: 85.8 us -> 82.6 us  [on_device(): pl.pallas_call(functools.partial(exchange_kernel, experts, rest, fold, s_...]
where the time goes in v4:
time: 85.3 us; the launch traced here: 85.2 us
  Pallas kernels  84.5 us (99%)
    pallas_call x1, Pallas kernels, on_device(): pl.pallas_call(functools.partial(exchange_kernel, experts, rest, fold, s_...  82.6 us
    pallas_call x1, Pallas kernels, on_device(): pl.pallas_call(store_kernel, out_shape=[jax.ShapeDtypeStruct(a.shape, a.d...  1.96 us

profile of v4, /device:TPU:0, one launch (start us, length us, event | category | flops | bytes accessed | tf_op | source)
XLA Modules:
  0.0 85.2 jit_solution(10288314023619549598)
XLA Ops:
  0.6 82.6 %shard_map.76 = (bf16[128,2,1536]{2,1,0:T(2,128)(2,1)S(1)}, bf16[2,128]{1,0:T(2,128)(2,1)S(1)}, bf16[768,2048]{1,0:T(8,128)(2,1)S(1)}) custom-call(s32[2,128]{1,0:T(2,128)} %bitcast.6, bf16[2,128]{1,0:T(2,128)(2,1)} %bitcast.7, bf16[128,4096]{1,0:T(8,128)(2,1)} %rows_hbm.1, bf16[128,2,1536]{2,1,0:T(2,128)(2,1)} %saved_hbm.1, bf16[768,2048]{1,0:T(8,128)(2,1)} %bitcast.5), custom_call_target="tpu_custom_call" | custom-call | tf_op jit(solution)/shard_map/pallas_call | solution.py:653
  83.2 2.0 %shard_map.77 = (bf16[128,2,1536]{2,1,0:T(2,128)(2,1)}, bf16[2,128]{1,0:T(2,128)(2,1)}, bf16[768,2048]{1,0:T(8,128)(2,1)}) custom-call(bf16[128,2,1536]{2,1,0:T(2,128)(2,1)S(1)} %get-tuple-element.9.refs_0_, bf16[2,128]{1,0:T(2,128)(2,1)S(1)} %get-tuple-element.10.refs_1_, bf16[768,2048]{1,0:T(8,128)(2,1)S(1)} %get-tuple-element.11.refs_2_), custom_call_target="tpu_custom_call" | custom-call | tf_op jit(solution)/shard_map/pallas_call | solution.py:711

commit v5 on v4

--- a/solution.py
+++ b/solution.py
@@ -232,7 +232,7 @@
             (other if side == 0 else d, near + j),
         )
 
-    chunk, ahead, lead = half // chunks, 8, 5
+    chunk, ahead, lead = half // chunks, 8, 6
     order = [(0, n) for n in range(lead)]
     for n in range(chunks):
         order += [(0, n + lead)] * (n + lead < chunks) + [(1, n)]
@@ -485,15 +485,15 @@
     pltpu.make_async_copy(
         s_pack.at[block(half_experts + at)], s.at[block(3 * half_experts + at)], rss.at[0]
     ).start()
-    raw_steps(0, 4)
+    raw_steps(0, 6)
     each_near(start_near_across)
-    raw_steps(4, 8)
+    raw_steps(6, 8)
     wait_bytes(s.at[rows_of(3)], rss.at[0])
     forward_near().start()
     raw_steps(8, 14)
-    send_partial(1)
     send_partial(0)
     raw_steps(14, 16)
+    send_partial(1)
     scaled_start(True)
     finish(0)
     def start_back_far(k):

time: 85.3 us -> 84.4 us (0.989)
  Pallas kernels: 84.5 us -> 83.6 us
    pallas_call x1, Pallas kernels: 82.6 us -> 81.6 us  [on_device(): pl.pallas_call(functools.partial(exchange_kernel, experts, rest, fold, s_...]
where the time goes in v5:
time: 84.4 us; the launch traced here: 84.2 us
  Pallas kernels  83.6 us (99%)
    pallas_call x1, Pallas kernels, on_device(): pl.pallas_call(functools.partial(exchange_kernel, experts, rest, fold, s_...  81.6 us
    pallas_call x1, Pallas kernels, on_device(): pl.pallas_call(store_kernel, out_shape=[jax.ShapeDtypeStruct(a.shape, a.d...  1.96 us

profile of v5, /device:TPU:0, one launch (start us, length us, event | category | flops | bytes accessed | tf_op | source)
XLA Modules:
  0.0 84.2 jit_solution(1736093096305882351)
XLA Ops:
  0.6 81.6 %shard_map.76 = (bf16[128,2,1536]{2,1,0:T(2,128)(2,1)S(1)}, bf16[2,128]{1,0:T(2,128)(2,1)S(1)}, bf16[768,2048]{1,0:T(8,128)(2,1)S(1)}) custom-call(s32[2,128]{1,0:T(2,128)} %bitcast.6, bf16[2,128]{1,0:T(2,128)(2,1)} %bitcast.7, bf16[128,4096]{1,0:T(8,128)(2,1)} %rows_hbm.1, bf16[128,2,1536]{2,1,0:T(2,128)(2,1)} %saved_hbm.1, bf16[768,2048]{1,0:T(8,128)(2,1)} %bitcast.5), custom_call_target="tpu_custom_call" | custom-call | tf_op jit(solution)/shard_map/pallas_call | solution.py:653
  82.2 2.0 %shard_map.77 = (bf16[128,2,1536]{2,1,0:T(2,128)(2,1)}, bf16[2,128]{1,0:T(2,128)(2,1)}, bf16[768,2048]{1,0:T(8,128)(2,1)}) custom-call(bf16[128,2,1536]{2,1,0:T(2,128)(2,1)S(1)} %get-tuple-element.9.refs_0_, bf16[2,128]{1,0:T(2,128)(2,1)S(1)} %get-tuple-element.10.refs_1_, bf16[768,2048]{1,0:T(8,128)(2,1)S(1)} %get-tuple-element.11.refs_2_), custom_call_target="tpu_custom_call" | custom-call | tf_op jit(solution)/shard_map/pallas_call | solution.py:711

commit v6 on v5

--- a/solution.py
+++ b/solution.py
@@ -485,12 +485,11 @@
     pltpu.make_async_copy(
         s_pack.at[block(half_experts + at)], s.at[block(3 * half_experts + at)], rss.at[0]
     ).start()
-    raw_steps(0, 6)
+    raw_steps(0, 7)
     each_near(start_near_across)
-    raw_steps(6, 8)
     wait_bytes(s.at[rows_of(3)], rss.at[0])
     forward_near().start()
-    raw_steps(8, 14)
+    raw_steps(7, 14)
     send_partial(0)
     raw_steps(14, 16)
     send_partial(1)

time: 84.4 us -> 84.4 us (level)
  no operation moved by 1% of the time
where the time goes in v6:
time: 84.4 us; the launch traced here: 84.2 us
  Pallas kernels  83.6 us (99%)
    pallas_call x1, Pallas kernels, on_device(): pl.pallas_call(functools.partial(exchange_kernel, experts, rest, fold, s_...  81.6 us
    pallas_call x1, Pallas kernels, on_device(): pl.pallas_call(store_kernel, out_shape=[jax.ShapeDtypeStruct(a.shape, a.d...  1.96 us

profile of v6, /device:TPU:0, one launch (start us, length us, event | category | flops | bytes accessed | tf_op | source)
XLA Modules:
  0.0 84.2 jit_solution(15683195250222099985)
XLA Ops:
  0.6 81.6 %shard_map.76 = (bf16[128,2,1536]{2,1,0:T(2,128)(2,1)S(1)}, bf16[2,128]{1,0:T(2,128)(2,1)S(1)}, bf16[768,2048]{1,0:T(8,128)(2,1)S(1)}) custom-call(s32[2,128]{1,0:T(2,128)} %bitcast.6, bf16[2,128]{1,0:T(2,128)(2,1)} %bitcast.7, bf16[128,4096]{1,0:T(8,128)(2,1)} %rows_hbm.1, bf16[128,2,1536]{2,1,0:T(2,128)(2,1)} %saved_hbm.1, bf16[768,2048]{1,0:T(8,128)(2,1)} %bitcast.5), custom_call_target="tpu_custom_call" | custom-call | tf_op jit(solution)/shard_map/pallas_call | solution.py:652
  82.3 2.0 %shard_map.77 = (bf16[128,2,1536]{2,1,0:T(2,128)(2,1)}, bf16[2,128]{1,0:T(2,128)(2,1)}, bf16[768,2048]{1,0:T(8,128)(2,1)}) custom-call(bf16[128,2,1536]{2,1,0:T(2,128)(2,1)S(1)} %get-tuple-element.9.refs_0_, bf16[2,128]{1,0:T(2,128)(2,1)S(1)} %get-tuple-element.10.refs_1_, bf16[768,2048]{1,0:T(8,128)(2,1)S(1)} %get-tuple-element.11.refs_2_), custom_call_target="tpu_custom_call" | custom-call | tf_op jit(solution)/shard_map/pallas_call | solution.py:710
